TPU v7x, 256 devices: a whole 4x4x8 slice. The times are simulated.
256 devices in a mesh: gx: 4 (over x_lo, core), gy: 8 (over x_hi, y), gz: 8 (over z).
Axes of the slice: x: 4 (x_hi: 2, x_lo: 2; x = x_hi * 2 + x_lo), y: 4, z: 8, core: 2. Of those that a mesh axis runs over, the one named last changes fastest.
Arguments:
- hamiltonian: float32 [4, 8, 8, 7, 384, 384], P('gx', 'gy', 'gz'), may hold values from -20 to 20, as said below
- keep_mask: int32 [4, 8, 8, 7], P('gx', 'gy', 'gz'), may hold values from 0 to 1, as said below
Outputs:
- sign_blocks: float32 [4, 8, 8, 7, 384, 384], P('gx', 'gy', 'gz')
Inputs may be any that keep to these rules, and one draw needn't show every extreme that they name: `hamiltonian`: entries are real numbers; the blocks are dense. `keep_mask`: slot 0 is 1 for every domain.
All inputs are finite; a program needn't handle non-finite values.
Results may differ from a plain program's by a relative error of at most 0.00025.
Values sent between devices are 32-bit elements; how exact they have to be, the bound alone decides.
A program may use at most 128 MiB of HBM per device.

v0:
```python
import jax
import jax.numpy as jnp
from jax import lax
from jax.sharding import PartitionSpec as P

HIGHEST = lax.Precision.HIGHEST
TARGET_RMS = 1.0


def with_halo(cells, sides, width):
    for axis, dim in sides:
        count = lax.axis_size(axis)
        head = lax.slice_in_dim(cells, 0, width, axis=dim)
        tail = lax.slice_in_dim(cells, cells.shape[dim] - width, cells.shape[dim], axis=dim)
        cells = jnp.concatenate(
            [
                lax.ppermute(tail, axis, [(i, (i + 1) % count) for i in range(count)]),
                cells,
                lax.ppermute(head, axis, [((i + 1) % count, i) for i in range(count)]),
            ],
            axis=dim,
        )
    return cells


def passed_along(value, axis, steps):
    count = lax.axis_size(axis)
    pairs = [(source, (source + steps) % count) for source in range(count)]
    return lax.ppermute(value, axis, pairs)


def gather_faces(stack):
    padded = with_halo(stack[0][None, None, None], (("gx", 0), ("gy", 1), ("gz", 2)), 1)
    return jnp.stack(
        [
            padded[2, 1, 1],
            padded[0, 1, 1],
            padded[1, 2, 1],
            padded[1, 0, 1],
            padded[1, 1, 2],
            padded[1, 1, 0],
        ]
    )


def gather_partners(stack, keep):
    next_x, keep_nx = passed_along((stack[2], keep[2]), "gx", -1)
    prev_x, keep_px = passed_along((stack[1], keep[1]), "gx", 1)
    next_y, keep_ny = passed_along((stack[4], keep[4]), "gy", -1)
    prev_y, keep_py = passed_along((stack[3], keep[3]), "gy", 1)
    next_z, keep_nz = passed_along((stack[6], keep[6]), "gz", -1)
    prev_z, keep_pz = passed_along((stack[5], keep[5]), "gz", 1)
    partners = jnp.stack([next_x, prev_x, next_y, prev_y, next_z, prev_z])
    near_keep = jnp.stack([keep_nx, keep_px, keep_ny, keep_py, keep_nz, keep_pz])
    return (partners, near_keep)


def product(left, right, faces, partners):
    centre = jnp.dot(left[0], right[0], precision=HIGHEST) + jnp.einsum(
        "sij,sjk->ik", left[1:], partners, precision=HIGHEST
    )
    others = jnp.einsum("ij,sjk->sik", left[0], right[1:], precision=HIGHEST) + jnp.einsum(
        "sij,sjk->sik", left[1:], faces, precision=HIGHEST
    )
    return jnp.concatenate([centre[None], others], axis=0)


def body(hamiltonian, keep_mask):
    blocks = hamiltonian[0, 0, 0]
    keep = keep_mask[0, 0, 0].astype(jnp.float32)
    weights = keep[:, None, None]
    width = blocks.shape[-1]
    entry_count = lax.axis_size("gx") * lax.axis_size("gy") * lax.axis_size("gz") * width
    own_squares = jnp.sum(blocks * blocks)
    sum_total = lax.psum(own_squares, ("gx", "gy", "gz"))
    factor = TARGET_RMS / jnp.sqrt(sum_total / entry_count)
    iterate = factor * blocks
    faces = gather_faces(iterate)
    partners, near_keep = gather_partners(iterate, keep)
    square = weights * product(iterate, iterate, faces, partners)
    square_faces = gather_faces(square)
    square_partners, unused = gather_partners(square, keep)
    cube = product(iterate, square, square_faces, square_partners)
    iterate = weights * (1.5 * iterate - 0.5 * cube)
    return iterate[None, None, None]


def solution(mesh):
    placed = (P("gx", "gy", "gz", None, None, None), P("gx", "gy", "gz", None))
    return jax.shard_map(
        body,
        mesh=mesh,
        in_specs=placed,
        out_specs=P("gx", "gy", "gz", None, None, None),
        check_vma=False,
    )
```

profile of v0, /device:TPU:1, one launch (start us, length us, event | category | flops | bytes accessed | tf_op | source)
XLA Modules:
  0.0 512.7 jit_solution(6742761087101006873)
XLA Ops:
  0.0 3.8 multiply_reduce_fusion
  3.8 81.4 %psum.7 = f32[]{:T(128)} all-reduce(f32[]{:T(128)} %multiply_reduce_fusion), channel_id=1, replica_groups=mesh['gx'=4,'gy'=8,'gz'=8] {'gx','gy','gz'}, use_global_device_ids=true, to_apply=%region_1.0 | all-reduce | flops 1 | bytes 8 | tf_op jit(solution)/shard_map/psum | solution.py:75
  85.9 2.5 broadcast_multiply_fusion
  88.8 1.0 collective-permute-start.6
  89.8 9.2 %collective-permute-done.7 = f32[1,1,1,384,384]{4,3,2,1,0:T(8,128)S(1)} collective-permute-done((f32[1,1,1,384,384]{4,3,2,1,0:T(8,128)S(1)}, f32[1,1,1,384,384]{4,3,2,1,0:T(8,128)S(1)}, u32[]{:S(2)}, u32[]{:S(2)}) %collective-permute-start.7) | collective-permute-done | bytes 589856 | tf_op jit(solution)/shard_map/ppermute | solution.py:17
  99.0 5.6 %collective-permute-done.6 = f32[1,1,1,384,384]{4,3,2,1,0:T(8,128)S(1)} collective-permute-done((f32[1,1,1,384,384]{4,3,2,1,0:T(8,128)S(1)}, f32[1,1,1,384,384]{4,3,2,1,0:T(8,128)S(1)}, u32[]{:S(2)}, u32[]{:S(2)}) %collective-permute-start.6) | collective-permute-done | bytes 589856 | tf_op jit(solution)/shard_map/ppermute | solution.py:19
  104.9 5.1 collective-permute-start.8
  109.9 38.1 %collective-permute-done.9 = f32[3,1,1,384,384]{4,3,2,1,0:T(8,128)S(1)} collective-permute-done((f32[3,1,1,384,384]{4,3,2,1,0:T(8,128)S(1)}, f32[3,1,1,384,384]{4,3,2,1,0:T(8,128)S(1)}, u32[]{:S(2)}, u32[]{:S(2)}) %collective-permute-start.9) | collective-permute-done | bytes 1769504 | tf_op jit(solution)/shard_map/ppermute | solution.py:17
  148.1 2.6 pad_maximum_fusion
  150.9 0.9 collective-permute-start.10
  152.4 4.7 collective-permute-start.2
  157.1 2.0 collective-permute-start.1
  159.1 1.1 collective-permute-start
  160.2 11.2 %fusion.6 = f32[6,384,384]{2,1,0:T(8,128)S(1)} fusion(f32[1,1,1,7,384,384]{5,4,3,2,1,0:T(8,128)S(1)} %broadcast_multiply_fusion), kind=kOutput, calls=%fused_computation.14 | convolution fusion | flops 4076863488 | bytes 7667712 | tf_op jit(solution)/shard_map/ij,sjk->sik/dot_general | solution.py:62
  171.5 1.5 fusion.28
  173.0 10.8 %collective-permute-done = f32[384,384]{1,0:T(8,128)S(1)} collective-permute-done((f32[384,384]{1,0:T(8,128)S(1)}, f32[384,384]{1,0:T(8,128)S(1)}, u32[]{:S(2)}, u32[]{:S(2)}) %collective-permute-start) | collective-permute-done | bytes 589856 | tf_op jit(solution)/shard_map/ppermute | solution.py:29
  183.8 1.8 collective-permute-start.4
  185.8 16.9 %collective-permute-done.3 = f32[384,384]{1,0:T(8,128)S(1)} collective-permute-done((f32[384,384]{1,0:T(8,128)S(1)}, f32[384,384]{1,0:T(8,128)S(1)}, u32[]{:S(2)}, u32[]{:S(2)}) %collective-permute-start.3) | collective-permute-done | bytes 589856 | tf_op jit(solution)/shard_map/ppermute | solution.py:29
  202.7 75.7 %collective-permute-done.4 = f32[384,384]{1,0:T(8,128)S(1)} collective-permute-done((f32[384,384]{1,0:T(8,128)S(1)}, f32[384,384]{1,0:T(8,128)S(1)}, u32[]{:S(2)}, u32[]{:S(2)}) %collective-permute-start.4) | collective-permute-done | bytes 589856 | tf_op jit(solution)/shard_map/ppermute | solution.py:29
  278.4 1.9 collective-permute-done.5
  280.4 6.6 %fusion.13 = f32[1,384,384]{2,1,0:T(8,128)} fusion(f32[384,384]{1,0:T(8,128)S(1)} %fusion.28, f32[6,384,384]{2,1,0:T(8,128)S(1)} %bitcast_dynamic-update-slice_fusion.10, f32[1,1,1,7,384,384]{5,4,3,2,1,0:T(8,128)S(1)} %broadcast_multiply_fusion), kind=kOutput, calls=%fused_computation.24 | convolution fusion | flops 4077010944 | bytes 8257536 | tf_op jit(solution)/shard_map/sij,sjk->ik/dot_general | solution.py:59
  287.0 2.1 copy.5
  289.1 1.3 bitcast_dynamic-update-slice_fusion.9
  290.3 1.3 bitcast_dynamic-update-slice_fusion.8
  291.6 1.1 fusion.21
  292.7 1.1 fusion.20
  293.8 1.1 fusion.19
  294.9 1.1 fusion.18
  296.1 7.9 %bitcast_add_fusion.1 = f32[6,384,384]{1,2,0:T(8,128)S(1)} fusion(f32[6,384,384]{2,1,0:T(8,128)S(1)} %fusion.6, f32[6,384,384]{2,1,0:T(8,128)S(1)} %fusion.18, f32[1,1,1,7,384,384]{5,4,3,2,1,0:T(8,128)S(1)} %copy-done.1), kind=kOutput, calls=%fused_computation.10 | convolution fusion | flops 4077748224 | bytes 14155776 | tf_op jit(solution)/shard_map/sij,sjk->sik/dot_general | solution.py:62
  304.6 2.0 collective-permute-start.19
  306.6 0.7 collective-permute-start.18
  307.3 9.9 %collective-permute-done.19 = f32[1,1,1,384,384]{3,4,2,1,0:T(8,128)S(1)} collective-permute-done((f32[1,1,1,384,384]{3,4,2,1,0:T(8,128)S(1)}, f32[1,1,1,384,384]{3,4,2,1,0:T(8,128)S(1)}, u32[]{:S(2)}, u32[]{:S(2)}) %collective-permute-start.19) | collective-permute-done | bytes 589856 | tf_op jit(solution)/shard_map/ppermute | solution.py:17
  317.2 5.1 collective-permute-done.18
  322.5 5.1 collective-permute-start.20
  327.6 38.3 %collective-permute-done.21 = f32[3,1,1,384,384]{3,4,2,1,0:T(8,128)S(1)} collective-permute-done((f32[3,1,1,384,384]{3,4,2,1,0:T(8,128)S(1)}, f32[3,1,1,384,384]{3,4,2,1,0:T(8,128)S(1)}, u32[]{:S(2)}, u32[]{:S(2)}) %collective-permute-start.21) | collective-permute-done | bytes 1769504 | tf_op jit(solution)/shard_map/ppermute | solution.py:17
  366.5 1.4 collective-permute-start.23
  367.9 2.2 collective-permute-start.12
  370.1 6.0 %fusion.22 = f32[6,384,384]{1,2,0:T(8,128)S(1)} fusion(f32[7,384,384]{1,2,0:T(8,128)S(1)} %maximum_multiply_fusion, f32[1,1,1,7,384,384]{5,4,3,2,1,0:T(8,128)S(1)} %copy-done.1), kind=kOutput, calls=%fused_computation.55 | convolution fusion | flops 4076863488 | bytes 8257536 | tf_op jit(solution)/shard_map/ij,sjk->sik/dot_general | solution.py:62
  376.3 1.3 fusion.25
  378.0 5.5 %collective-permute-start.14 = (f32[384,384]{0,1:T(8,128)S(1)}, f32[384,384]{0,1:T(8,128)S(1)}, u32[]{:S(2)}, u32[]{:S(2)}) collective-permute-start(f32[384,384]{0,1:T(8,128)S(1)} %get-tuple-element.9), channel_id=1, source_target_pairs={{0,56},{8,0},{16,8},{24,16},{32,24},{40,32},{48,40},{56,48},{1,57}... | collective-permute-start | bytes 1769480 | tf_op jit(solution)/shard_map/ppermute | solution.py:29
  383.6 1.4 collective-permute-start.16
  385.0 11.4 %collective-permute-done.14 = f32[384,384]{0,1:T(8,128)S(1)} collective-permute-done((f32[384,384]{0,1:T(8,128)S(1)}, f32[384,384]{0,1:T(8,128)S(1)}, u32[]{:S(2)}, u32[]{:S(2)}) %collective-permute-start.14) | collective-permute-done | bytes 589856 | tf_op jit(solution)/shard_map/ppermute | solution.py:29
  396.9 96.9 %collective-permute-done.16 = f32[384,384]{0,1:T(8,128)S(1)} collective-permute-done((f32[384,384]{0,1:T(8,128)S(1)}, f32[384,384]{0,1:T(8,128)S(1)}, u32[]{:S(2)}, u32[]{:S(2)}) %collective-permute-start.16) | collective-permute-done | bytes 589856 | tf_op jit(solution)/shard_map/ppermute | solution.py:29
  493.8 1.0 collective-permute-done.17
  494.9 5.9 %fusion.11 = f32[1,1,1,1,384,384]{5,4,3,2,1,0:T(8,128)S(1)} fusion(f32[384,384]{1,0:T(8,128)S(1)} %fusion.25, f32[6,384,384]{1,2,0:T(8,128)S(1)} %bitcast_dynamic-update-slice_fusion.2, f32[1,1,1,7,384,384]{5,4,3,2,1,0:T(8,128)S(1)} %copy-done.1), kind=kOutput, calls=%fused_computation.22 | convolution fusion | flops 4077010944 | bytes 8257536 | tf_op jit(solution)/shard_map/sij,sjk->ik/dot_general | solution.py:59
  500.9 1.1 fusion.15
  502.1 7.7 %fusion.2 = f32[1,1,1,6,384,384]{5,4,3,2,1,0:T(8,128)S(1)} fusion(f32[6,384,384]{1,2,0:T(8,128)S(1)} %fusion.22, f32[6,384,384]{1,2,0:T(8,128)S(1)} %fusion.14, f32[1,1,1,7,384,384]{5,4,3,2,1,0:T(8,128)S(1)} %copy-done.1), kind=kOutput, calls=%fused_computation.9 | convolution fusion | flops 4077748224 | bytes 14155776 | tf_op jit(solution)/shard_map/sij,sjk->sik/dot_general | solution.py:62
  509.8 2.7 fusion.1
  (63 shorter events, 4.4 us)
Async XLA Ops:
  88.4 191.9 %copy-start = (f32[1,1,1,7,384,384]{5,4,3,2,1,0:T(8,128)}, f32[1,1,1,7,384,384]{5,4,3,2,1,0:T(8,128)S(1)}, u32[]{:S(2)}) copy-start(f32[1,1,1,7,384,384]{5,4,3,2,1,0:T(8,128)S(1)} %broadcast_multiply_fusion) | copy-start | bytes 12386308
  88.7 10.3 %collective-permute-start.7 = (f32[1,1,1,384,384]{4,3,2,1,0:T(8,128)S(1)}, f32[1,1,1,384,384]{4,3,2,1,0:T(8,128)S(1)}, u32[]{:S(2)}, u32[]{:S(2)}) collective-permute-start(f32[1,1,1,384,384]{4,3,2,1,0:T(8,128)S(1)} %get-tuple-element.13), channel_id=1, source_target_pairs={{0,64},{64,128},{128,192},{192,0},{1,65},{65,129},{129,193},{193,1... | collective-permute-start | bytes 1769480 | tf_op jit(solution)/shard_map/ppermute | solution.py:17
  88.8 15.8 %collective-permute-start.6 = (f32[1,1,1,384,384]{4,3,2,1,0:T(8,128)S(1)}, f32[1,1,1,384,384]{4,3,2,1,0:T(8,128)S(1)}, u32[]{:S(2)}, u32[]{:S(2)}) collective-permute-start(f32[1,1,1,384,384]{4,3,2,1,0:T(8,128)S(1)} %get-tuple-element.13), channel_id=1, source_target_pairs={{64,0},{128,64},{192,128},{0,192},{65,1},{129,65},{193,129},{1,193... | collective-permute-start | bytes 1769480 | tf_op jit(solution)/shard_map/ppermute | solution.py:19
  99.0 72.4 %copy-start.3 = (f32[1,1,1,384,384]{4,3,2,1,0:T(8,128)}, f32[1,1,1,384,384]{4,3,2,1,0:T(8,128)S(1)}, u32[]{:S(2)}) copy-start(f32[1,1,1,384,384]{4,3,2,1,0:T(8,128)S(1)} %collective-permute-done.7) | copy-start | bytes 1769476
  104.6 66.8 %copy-start.4 = (f32[1,1,1,384,384]{4,3,2,1,0:T(8,128)}, f32[1,1,1,384,384]{4,3,2,1,0:T(8,128)S(1)}, u32[]{:S(2)}) copy-start(f32[1,1,1,384,384]{4,3,2,1,0:T(8,128)S(1)} %collective-permute-done.6) | copy-start | bytes 1769476
  104.8 43.3 %collective-permute-start.9 = (f32[3,1,1,384,384]{4,3,2,1,0:T(8,128)S(1)}, f32[3,1,1,384,384]{4,3,2,1,0:T(8,128)S(1)}, u32[]{:S(2)}, u32[]{:S(2)}) collective-permute-start(f32[3,1,1,384,384]{4,3,2,1,0:T(8,128)S(1)} %pad_maximum_fusion.2), channel_id=1, source_target_pairs={{0,8},{8,16},{16,24},{24,32},{32,40},{40,48},{48,56},{56,0},{1,9},... | collective-permute-start | bytes 5308424 | tf_op jit(solution)/shard_map/ppermute | solution.py:17
  104.9 43.2 %collective-permute-start.8 = (f32[3,1,1,384,384]{4,3,2,1,0:T(8,128)S(1)}, f32[3,1,1,384,384]{4,3,2,1,0:T(8,128)S(1)}, u32[]{:S(2)}, u32[]{:S(2)}) collective-permute-start(f32[3,1,1,384,384]{4,3,2,1,0:T(8,128)S(1)} %pad_maximum_fusion.2), channel_id=1, source_target_pairs={{8,0},{16,8},{24,16},{32,24},{40,32},{48,40},{56,48},{0,56},{9,1},... | collective-permute-start | bytes 5308424 | tf_op jit(solution)/shard_map/ppermute | solution.py:19
  148.1 37.6 %copy-start.5 = (f32[3,1,1,384,384]{4,3,2,1,0:T(8,128)}, f32[3,1,1,384,384]{4,3,2,1,0:T(8,128)S(1)}, u32[]{:S(2)}) copy-start(f32[3,1,1,384,384]{4,3,2,1,0:T(8,128)S(1)} %collective-permute-done.9) | copy-start | bytes 5308420
  148.1 2.9 copy-start.6
  150.9 142.9 %collective-permute-start.10 = (f32[3,3,1,384,384]{4,3,2,1,0:T(8,128)}, f32[3,3,1,384,384]{4,3,2,1,0:T(8,128)}, u32[]{:S(2)}, u32[]{:S(2)}) collective-permute-start(f32[3,3,1,384,384]{4,3,2,1,0:T(8,128)} %pad_maximum_fusion), channel_id=1, source_target_pairs={{1,0},{2,1},{3,2},{4,3},{5,4},{6,5},{7,6},{0,7},{9,8},{10,9},{11,1... | collective-permute-start | bytes 15925256 | tf_op jit(solution)/shard_map/ppermute | solution.py:19
  151.9 143.1 %collective-permute-start.11 = (f32[3,3,1,384,384]{4,3,2,1,0:T(8,128)}, f32[3,3,1,384,384]{4,3,2,1,0:T(8,128)}, u32[]{:S(2)}, u32[]{:S(2)}) collective-permute-start(f32[3,3,1,384,384]{4,3,2,1,0:T(8,128)} %pad_maximum_fusion), channel_id=1, source_target_pairs={{0,1},{1,2},{2,3},{3,4},{4,5},{5,6},{6,7},{7,0},{8,9},{9,10},{10,1... | collective-permute-start | bytes 15925256 | tf_op jit(solution)/shard_map/ppermute | solution.py:17
  152.4 33.2 %collective-permute-start.2 = (f32[384,384]{1,0:T(8,128)S(1)}, f32[384,384]{1,0:T(8,128)S(1)}, u32[]{:S(2)}, u32[]{:S(2)}) collective-permute-start(f32[384,384]{1,0:T(8,128)S(1)} %get-tuple-element.16), channel_id=1, source_target_pairs={{0,56},{8,0},{16,8},{24,16},{32,24},{40,32},{48,40},{56,48},{1,57}... | collective-permute-start | bytes 1769480 | tf_op jit(solution)/shard_map/ppermute | solution.py:29
  157.1 26.6 %collective-permute-start.1 = (f32[384,384]{1,0:T(8,128)S(1)}, f32[384,384]{1,0:T(8,128)S(1)}, u32[]{:S(2)}, u32[]{:S(2)}) collective-permute-start(f32[384,384]{1,0:T(8,128)S(1)} %get-tuple-element.17), channel_id=1, source_target_pairs={{0,64},{64,128},{128,192},{192,0},{1,65},{65,129},{129,193},{193,1... | collective-permute-start | bytes 1769480 | tf_op jit(solution)/shard_map/ppermute | solution.py:29
  159.1 13.8 %copy-start.8 = (s32[1,1,1,7]{3,2,1,0:T(1,128)S(1)}, s32[1,1,1,7]{3,2,1,0:T(1,128)}, u32[]{:S(2)}) copy-start(s32[1,1,1,7]{3,2,1,0:T(1,128)} %param.3) | copy-start | bytes 88
  159.1 24.6 %collective-permute-start = (f32[384,384]{1,0:T(8,128)S(1)}, f32[384,384]{1,0:T(8,128)S(1)}, u32[]{:S(2)}, u32[]{:S(2)}) collective-permute-start(f32[384,384]{1,0:T(8,128)S(1)} %get-tuple-element.18), channel_id=1, source_target_pairs={{0,192},{64,0},{128,64},{192,128},{1,193},{65,1},{129,65},{193,129... | collective-permute-start | bytes 1769480 | tf_op jit(solution)/shard_map/ppermute | solution.py:29
  183.7 18.9 %collective-permute-start.3 = (f32[384,384]{1,0:T(8,128)S(1)}, f32[384,384]{1,0:T(8,128)S(1)}, u32[]{:S(2)}, u32[]{:S(2)}) collective-permute-start(f32[384,384]{1,0:T(8,128)S(1)} %get-tuple-element.15), channel_id=1, source_target_pairs={{0,8},{8,16},{16,24},{24,32},{32,40},{40,48},{48,56},{56,0},{1,9},... | collective-permute-start | bytes 1769480 | tf_op jit(solution)/shard_map/ppermute | solution.py:29
  183.8 94.5 %collective-permute-start.4 = (f32[384,384]{1,0:T(8,128)S(1)}, f32[384,384]{1,0:T(8,128)S(1)}, u32[]{:S(2)}, u32[]{:S(2)}) collective-permute-start(f32[384,384]{1,0:T(8,128)S(1)} %get-tuple-element.14), channel_id=1, source_target_pairs={{0,7},{1,0},{2,1},{3,2},{4,3},{5,4},{6,5},{7,6},{8,15},{9,8},{10,9... | collective-permute-start | bytes 1769480 | tf_op jit(solution)/shard_map/ppermute | solution.py:29
  185.6 94.7 %collective-permute-start.5 = (f32[384,384]{1,0:T(8,128)S(1)}, f32[384,384]{1,0:T(8,128)S(1)}, u32[]{:S(2)}, u32[]{:S(2)}) collective-permute-start(f32[384,384]{1,0:T(8,128)S(1)} %get-tuple-element.12), channel_id=1, source_target_pairs={{0,1},{1,2},{2,3},{3,4},{4,5},{5,6},{6,7},{7,0},{8,9},{9,10},{10,1... | collective-permute-start | bytes 1769480 | tf_op jit(solution)/shard_map/ppermute | solution.py:29
  289.1 7.0 %copy-start.1 = (f32[1,1,1,7,384,384]{5,4,3,2,1,0:T(8,128)S(1)}, f32[1,1,1,7,384,384]{5,4,3,2,1,0:T(8,128)}, u32[]{:S(2)}) copy-start(f32[1,1,1,7,384,384]{5,4,3,2,1,0:T(8,128)} %copy-done) | copy-start | bytes 12386308
  296.1 7.9 %copy-start.7 = (f32[1,384,384]{1,2,0:T(8,128)S(1)}, f32[1,384,384]{1,2,0:T(8,128)}, u32[]{:S(2)}) copy-start(f32[1,384,384]{1,2,0:T(8,128)} %copy.5) | copy-start | bytes 1769476
  304.6 12.6 %collective-permute-start.19 = (f32[1,1,1,384,384]{3,4,2,1,0:T(8,128)S(1)}, f32[1,1,1,384,384]{3,4,2,1,0:T(8,128)S(1)}, u32[]{:S(2)}, u32[]{:S(2)}) collective-permute-start(f32[1,1,1,384,384]{3,4,2,1,0:T(8,128)S(1)} %get-tuple-element.6), channel_id=1, source_target_pairs={{0,64},{64,128},{128,192},{192,0},{1,65},{65,129},{129,193},{193,1... | collective-permute-start | bytes 1769480 | tf_op jit(solution)/shard_map/ppermute | solution.py:17
  306.6 15.7 %collective-permute-start.18 = (f32[1,1,1,384,384]{3,4,2,1,0:T(8,128)S(1)}, f32[1,1,1,384,384]{3,4,2,1,0:T(8,128)S(1)}, u32[]{:S(2)}, u32[]{:S(2)}) collective-permute-start(f32[1,1,1,384,384]{3,4,2,1,0:T(8,128)S(1)} %get-tuple-element.6), channel_id=1, source_target_pairs={{64,0},{128,64},{192,128},{0,192},{65,1},{129,65},{193,129},{1,193... | collective-permute-start | bytes 1769480 | tf_op jit(solution)/shard_map/ppermute | solution.py:19
  322.4 43.5 %collective-permute-start.21 = (f32[3,1,1,384,384]{3,4,2,1,0:T(8,128)S(1)}, f32[3,1,1,384,384]{3,4,2,1,0:T(8,128)S(1)}, u32[]{:S(2)}, u32[]{:S(2)}) collective-permute-start(f32[3,1,1,384,384]{3,4,2,1,0:T(8,128)S(1)} %pad_maximum_fusion.3), channel_id=1, source_target_pairs={{0,8},{8,16},{16,24},{24,32},{32,40},{40,48},{48,56},{56,0},{1,9},... | collective-permute-start | bytes 5308424 | tf_op jit(solution)/shard_map/ppermute | solution.py:17
  322.5 43.4 %collective-permute-start.20 = (f32[3,1,1,384,384]{3,4,2,1,0:T(8,128)S(1)}, f32[3,1,1,384,384]{3,4,2,1,0:T(8,128)S(1)}, u32[]{:S(2)}, u32[]{:S(2)}) collective-permute-start(f32[3,1,1,384,384]{3,4,2,1,0:T(8,128)S(1)} %pad_maximum_fusion.3), channel_id=1, source_target_pairs={{8,0},{16,8},{24,16},{32,24},{40,32},{48,40},{56,48},{0,56},{9,1},... | collective-permute-start | bytes 5308424 | tf_op jit(solution)/shard_map/ppermute | solution.py:19
  366.3 134.5 %collective-permute-start.22 = (f32[3,3,1,384,384]{3,4,2,1,0:T(8,128)S(1)}, f32[3,3,1,384,384]{3,4,2,1,0:T(8,128)}, u32[]{:S(2)}, u32[]{:S(2)}) collective-permute-start(f32[3,3,1,384,384]{3,4,2,1,0:T(8,128)S(1)} %pad_maximum_fusion.1), channel_id=1, source_target_pairs={{1,0},{2,1},{3,2},{4,3},{5,4},{6,5},{7,6},{0,7},{9,8},{10,9},{11,1... | collective-permute-start | bytes 15925256 | tf_op jit(solution)/shard_map/ppermute | solution.py:19
  366.5 135.5 %collective-permute-start.23 = (f32[3,3,1,384,384]{3,4,2,1,0:T(8,128)S(1)}, f32[3,3,1,384,384]{3,4,2,1,0:T(8,128)S(1)}, u32[]{:S(2)}, u32[]{:S(2)}) collective-permute-start(f32[3,3,1,384,384]{3,4,2,1,0:T(8,128)S(1)} %pad_maximum_fusion.1), channel_id=1, source_target_pairs={{0,1},{1,2},{2,3},{3,4},{4,5},{5,6},{6,7},{7,0},{8,9},{9,10},{10,1... | collective-permute-start | bytes 15925256 | tf_op jit(solution)/shard_map/ppermute | solution.py:17
  367.9 10.1 %collective-permute-start.12 = (f32[384,384]{0,1:T(8,128)S(1)}, f32[384,384]{0,1:T(8,128)S(1)}, u32[]{:S(2)}, u32[]{:S(2)}) collective-permute-start(f32[384,384]{0,1:T(8,128)S(1)} %get-tuple-element.11), channel_id=1, source_target_pairs={{0,192},{64,0},{128,64},{192,128},{1,193},{65,1},{129,65},{193,129... | collective-permute-start | bytes 1769480 | tf_op jit(solution)/shard_map/ppermute | solution.py:29
  376.1 20.7 %collective-permute-start.15 = (f32[384,384]{0,1:T(8,128)S(1)}, f32[384,384]{0,1:T(8,128)S(1)}, u32[]{:S(2)}, u32[]{:S(2)}) collective-permute-start(f32[384,384]{0,1:T(8,128)S(1)} %get-tuple-element.8), channel_id=1, source_target_pairs={{0,8},{8,16},{16,24},{24,32},{32,40},{40,48},{48,56},{56,0},{1,9},... | collective-permute-start | bytes 1769480 | tf_op jit(solution)/shard_map/ppermute | solution.py:29
  376.2 7.4 %collective-permute-start.13 = (f32[384,384]{0,1:T(8,128)S(1)}, f32[384,384]{0,1:T(8,128)S(1)}, u32[]{:S(2)}, u32[]{:S(2)}) collective-permute-start(f32[384,384]{0,1:T(8,128)S(1)} %get-tuple-element.10), channel_id=1, source_target_pairs={{0,64},{64,128},{128,192},{192,0},{1,65},{65,129},{129,193},{193,1... | collective-permute-start | bytes 1769480 | tf_op jit(solution)/shard_map/ppermute | solution.py:29
  378.0 18.5 %collective-permute-start.14 = (f32[384,384]{0,1:T(8,128)S(1)}, f32[384,384]{0,1:T(8,128)S(1)}, u32[]{:S(2)}, u32[]{:S(2)}) collective-permute-start(f32[384,384]{0,1:T(8,128)S(1)} %get-tuple-element.9), channel_id=1, source_target_pairs={{0,56},{8,0},{16,8},{24,16},{32,24},{40,32},{48,40},{56,48},{1,57}... | collective-permute-start | bytes 1769480 | tf_op jit(solution)/shard_map/ppermute | solution.py:29
  383.6 110.2 %collective-permute-start.16 = (f32[384,384]{0,1:T(8,128)S(1)}, f32[384,384]{0,1:T(8,128)S(1)}, u32[]{:S(2)}, u32[]{:S(2)}) collective-permute-start(f32[384,384]{0,1:T(8,128)S(1)} %get-tuple-element.7), channel_id=1, source_target_pairs={{0,7},{1,0},{2,1},{3,2},{4,3},{5,4},{6,5},{7,6},{8,15},{9,8},{10,9... | collective-permute-start | bytes 1769480 | tf_op jit(solution)/shard_map/ppermute | solution.py:29
  396.4 98.4 %collective-permute-start.17 = (f32[384,384]{0,1:T(8,128)S(1)}, f32[384,384]{0,1:T(8,128)S(1)}, u32[]{:S(2)}, u32[]{:S(2)}) collective-permute-start(f32[384,384]{0,1:T(8,128)S(1)} %get-tuple-element.5), channel_id=1, source_target_pairs={{0,1},{1,2},{2,3},{3,4},{4,5},{5,6},{6,7},{7,0},{8,9},{9,10},{10,1... | collective-permute-start | bytes 1769480 | tf_op jit(solution)/shard_map/ppermute | solution.py:29
  502.1 7.7 %copy-start.2 = (f32[1,1,1,7,384,384]{5,4,3,2,1,0:T(8,128)S(1)}, f32[1,1,1,7,384,384]{5,4,3,2,1,0:T(8,128)}, u32[]{:S(2)}) copy-start(f32[1,1,1,7,384,384]{5,4,3,2,1,0:T(8,128)} %param.2) | copy-start | bytes 12386308
where the time goes:
time: 522 us; the launch traced here: 513 us
  waiting for transfers between devices  321 us (61%)
  blocking collectives  81.4 us (16%)
  matrix products  48.1 us (9%)
  starting transfers between devices  36.4 us (7%)
  other arithmetic  12.6 us (2%)
  local copies, waits for them, and re-layouts  11.6 us (2%)
    ppermute x12, waiting for transfers between devices, passed_along(): return lax.ppermute(value, axis, pairs)  215 us
    ppermute x6, waiting for transfers between devices, with_halo(): lax.ppermute(tail, axis, [(i, (i + 1) % count) for i in range(count)])  95.6 us
    psum x1, blocking collectives, body(): sum_total = lax.psum(own_squares, ('gx', 'gy', 'gz'))  81.4 us
    ppermute x12, starting transfers between devices, passed_along(): return lax.ppermute(value, axis, pairs)  19.3 us
    dot_general x2, matrix products, product(): jnp.einsum('ij,sjk->sik', left[0], right[1:], precision=HIGHEST)  17.2 us
    dot_general x2, matrix products, product(): jnp.einsum('sij,sjk->sik', left[1:], faces, precision=HIGHEST)  15.6 us
    ppermute x6, starting transfers between devices, with_halo(): lax.ppermute(head, axis, [((i + 1) % count, i) for i in range(count)])  12.9 us
    dot_general x2, matrix products, product(): jnp.einsum('sij,sjk->ik', left[1:], partners, precision=HIGHEST)  12.5 us
  transfers between devices with their start and end apart: 24, of which 14 were waited for; matrix products, arithmetic and copies ran while one was open for 8% of the time, Pallas kernels for 0%

commit v1 on v0

v1 whole, which is shorter than its diff:
```python
import functools

import jax
import jax.numpy as jnp
from jax import lax
from jax.experimental import pallas as pl
from jax.experimental.pallas import tpu as pltpu
from jax.sharding import PartitionSpec as P

MESH = pl.DeviceIdType.MESH
F32 = jnp.float32
BF16 = jnp.bfloat16
CHUNKS = 3


def kernel(
    sizes,
    count,
    h_hbm,
    keep,
    out,
    h,
    near_c,
    near_o,
    squares,
    near_keep,
    left,
    couple,
    first,
    tmp_a,
    tmp_b,
    kept_sum,
    centre,
    scale_sq,
    scale,
    part_x,
    part_y,
    part_z,
    load_sem,
    keep_send,
    keep_recv,
    part_send,
    part_recv,
    c_send,
    c_recv,
    o_send,
    o_recv,
    s_send,
    s_recv,
):
    nx, ny, nz = sizes
    width = h.shape[-1]
    rows = width // CHUNKS
    a, g, z = (lax.axis_index(n) for n in ("gx", "gy", "gz"))
    half = ny // 2
    at_top = lax.rem(g, half) == half - 1
    at_bottom = lax.rem(g, half) == 0
    edge = at_top | at_bottom
    up_x, down_x = lax.rem(a + 1, nx), lax.rem(a + nx - 1, nx)
    up_y, down_y = lax.rem(g + 1, ny), lax.rem(g + ny - 1, ny)
    up_z, down_z = lax.rem(z + 1, nz), lax.rem(z + nz - 1, nz)
    device = [
        (up_x, g, z),
        (down_x, g, z),
        (a, up_y, z),
        (a, down_y, z),
        (a, g, up_z),
        (a, g, down_z),
    ]
    across = nx - 1 - a
    cross = 1 - lax.rem(a, 2)
    near = 1 - cross
    passed_on = {2: (across, up_y, z), 3: (across, down_y, z)}
    wraps = {2: at_top, 3: at_bottom}

    def chunk(c):
        return pl.ds(c * rows, rows)

    barrier = pltpu.get_barrier_semaphore()
    peers_x = [(lax.rem(a + k, nx), g, z) for k in range(1, nx)]
    peers_y = [(a, lax.rem(g + k, ny), z) for k in range(1, ny)]
    peers_z = [(a, g, lax.rem(z + k, nz)) for k in range(1, nz)]
    for peer in peers_x + peers_y + peers_z:
        pl.semaphore_signal(barrier, inc=1, device_id=peer, device_id_type=MESH)
    for d in (2, 3):

        @pl.when(wraps[d])
        def _():
            pl.semaphore_signal(
                barrier, inc=1, device_id=passed_on[d], device_id_type=MESH
            )

    loads = [
        pltpu.make_async_copy(h_hbm.at[s], h.at[s], load_sem.at[s]) for s in range(7)
    ]
    for load in loads:
        load.start()
    total = jnp.zeros((8, 128), F32)
    for s in range(7):
        loads[s].wait()
        block = h[s]
        squared = jnp.sum((block * block).reshape(width // 8, 8, width), axis=0)
        for j in range(width // 128):
            total = total + squared[:, j * 128 : (j + 1) * 128]
    part_x[a] = total
    pl.semaphore_wait(barrier, nx + ny + nz - 3 + jnp.where(edge, 1, 0))

    def part_copies(stage, buffer, me, peers):
        return [
            pltpu.make_async_remote_copy(
                src_ref=buffer.at[me],
                dst_ref=buffer.at[me],
                send_sem=part_send.at[stage],
                recv_sem=part_recv.at[stage],
                device_id=peer,
                device_id_type=MESH,
            )
            for peer in peers
        ]

    def part_wait(stage, buffer, n):
        copy = pltpu.make_async_remote_copy(
            src_ref=buffer.at[pl.ds(0, n - 1)],
            dst_ref=buffer.at[pl.ds(0, n - 1)],
            send_sem=part_send.at[stage],
            recv_sem=part_recv.at[stage],
            device_id=device[0],
            device_id_type=MESH,
        )
        copy.wait_send()
        copy.wait_recv()

    def keep_copy(d):
        return pltpu.make_async_remote_copy(
            src_ref=keep.at[1 + d],
            dst_ref=near_keep.at[d ^ 1],
            send_sem=keep_send.at[d],
            recv_sem=keep_recv.at[d ^ 1],
            device_id=device[d],
            device_id_type=MESH,
        )

    def couple_copy(d):
        return pltpu.make_async_remote_copy(
            src_ref=h_hbm.at[1 + d],
            dst_ref=near_c.at[d ^ 1],
            send_sem=c_send.at[d],
            recv_sem=c_recv.at[d ^ 1],
            device_id=device[d],
            device_id_type=MESH,
        )

    def own_copy(d, c, source, target, send, recv):
        return pltpu.make_async_remote_copy(
            src_ref=source.at[0, chunk(c)],
            dst_ref=target.at[1 + (d ^ 1), chunk(c)],
            send_sem=send.at[d, c],
            recv_sem=recv.at[d ^ 1, c],
            device_id=device[d],
            device_id_type=MESH,
        )

    def pass_copy(d, c, target, send, recv):
        return pltpu.make_async_remote_copy(
            src_ref=target.at[1 + cross, chunk(c)],
            dst_ref=target.at[1 + (d ^ 1), chunk(c)],
            send_sem=send.at[d, c],
            recv_sem=recv.at[d ^ 1, c],
            device_id=passed_on[d],
            device_id_type=MESH,
        )

    def arrival(d, c, target, send, recv):
        return pltpu.make_async_remote_copy(
            src_ref=target.at[1 + d, chunk(c)],
            dst_ref=target.at[1 + d, chunk(c)],
            send_sem=send.at[0, c],
            recv_sem=recv.at[d, c],
            device_id=device[0],
            device_id_type=MESH,
        )

    def send_own(source, target, send, recv):
        for c in range(CHUNKS):
            for d in range(6):
                copy = own_copy(d, c, source, target, send, recv)
                if d in wraps:
                    pl.when(jnp.logical_not(wraps[d]))(copy.start)
                else:
                    copy.start()

    def pass_chunk(c, target, send, recv):
        arrival(cross, c, target, send, recv).wait_recv()
        for d in (2, 3):
            pl.when(wraps[d])(pass_copy(d, c, target, send, recv).start)

    squares_copies = (squares, squares, s_send, s_recv)
    own_copies = (h_hbm, near_o, o_send, o_recv)

    stage_x = part_copies(0, part_x, a, peers_x)
    for copy in stage_x:
        copy.start()
    for d in range(6):
        keep_copy(d).start()
    for d in range(6):
        couple_copy(d).start()
    send_own(*own_copies)

    def parts(x):
        high = x.astype(BF16)
        return high, (x - high.astype(F32)).astype(BF16)

    def as_left(x, ref):
        for c in range(CHUNKS):
            high, low = parts(x[:, c * rows : (c + 1) * rows])
            base = 3 * c * rows
            ref[:, base : base + rows] = high
            ref[:, base + rows : base + 2 * rows] = high
            ref[:, base + 2 * rows : base + 3 * rows] = low

    def as_right_chunk(x, ref, base):
        high, low = parts(x)
        ref[pl.ds(base, rows)] = high
        ref[pl.ds(base + rows, rows)] = low
        ref[pl.ds(base + 2 * rows, rows)] = high

    def as_right(x, ref):
        for c in range(CHUNKS):
            as_right_chunk(x[c * rows : (c + 1) * rows], ref, 3 * c * rows)

    def mul(x, y):
        return jnp.dot(x, y, preferred_element_type=F32)

    as_left(h[0], left.at[0])
    as_right(h[0], first)

    @pl.loop(0, 7)
    def _(s):
        block = h[s]
        as_left(block, left.at[s])
        as_right(block, tmp_b)
        out[s] = mul(left[0], tmp_b[...])

    part_wait(0, part_x, nx)
    part_y[g] = jnp.sum(part_x[...], axis=0)
    for copy in part_copies(1, part_y, g, peers_y):
        copy.start()
    part_wait(1, part_y, ny)
    part_z[z] = jnp.sum(part_y[...], axis=0)
    for copy in part_copies(2, part_z, z, peers_z):
        copy.start()

    kept_sum[...] = jnp.zeros_like(kept_sum)
    for d in range(6):
        keep_copy(d).wait_recv()

    @pl.loop(0, 6)
    def _(p):
        d = jnp.where(p == 0, near, jnp.where(p == 5, cross, jnp.where(p < 3, p + 3, p - 1)))
        pltpu.make_async_remote_copy(
            src_ref=near_c.at[d],
            dst_ref=near_c.at[d],
            send_sem=c_send.at[0],
            recv_sem=c_recv.at[d],
            device_id=device[0],
            device_id_type=MESH,
        ).wait_recv()
        as_right(near_c[d], couple.at[d])
        both = mul(left[1 + d], couple[d])
        out[0] += both
        kept_sum[...] += near_keep[d, 0:1] * both

    part_wait(2, part_z, nz)
    norm = jnp.sum(jnp.sum(part_z[...], axis=0), keepdims=True)
    norm = jnp.broadcast_to(norm, (8, width)) / count
    factor_sq = 1.0 / norm
    factor = 1.0 / jnp.sqrt(norm)
    scale_sq[...] = factor_sq
    for s in range(7):
        scale[s] = factor * keep[s]
    squares[0] = (scale_sq[0:1] * keep[0, 0:1]) * out[0]
    send_own(*squares_copies)

    for c in range(CHUNKS):
        pass_chunk(c, near_o, o_send, o_recv)
    as_left(scale_sq[0:1] * kept_sum[...], tmp_a)
    centre[...] = mul(tmp_a[...], first[...])
    as_right(squares[0], tmp_b)
    centre[...] += mul(left[0], tmp_b[...])

    @pl.loop(0, 6)
    def _(p):
        d = jnp.where(p == 0, near, jnp.where(p == 1, cross, jnp.where(p < 4, p + 2, p - 2)))

        @pl.when(p != 1)
        def _():
            for c in range(CHUNKS):
                arrival(d, c, near_o, o_send, o_recv).wait_recv()

        as_right(near_o[1 + d], tmp_b)
        with_own = mul(left[1 + d], tmp_b[...])
        as_right((scale_sq[0:1] * keep[1 + d, 0:1]) * (out[1 + d] + with_own), tmp_b)
        as_left((scale_sq[0:1] * near_keep[d, 0:1]) * with_own, tmp_a)
        out[1 + d] = scale[1 + d, 0:1] * (1.5 * h[1 + d] - 0.5 * mul(left[0], tmp_b[...]))
        centre[...] += mul(tmp_a[...], couple[d])

    out[0] = scale[0, 0:1] * (1.5 * h[0] - 0.5 * centre[...])

    def finish(d, c):
        base = 3 * c * rows
        as_right_chunk(squares[1 + d, chunk(c)], tmp_b, base)
        out[1 + d] -= (0.5 * scale[1 + d, 0:1]) * mul(
            left[1 + d, :, base : base + 3 * rows], tmp_b[base : base + 3 * rows]
        )

    def finish_y(c):
        @pl.loop(2, 4)
        def _(d):
            arrival(d, c, squares, s_send, s_recv).wait_recv()
            finish(d, c)

    for c in range(CHUNKS):
        pass_chunk(c, squares, s_send, s_recv)

        @pl.loop(0, 4)
        def _(p):
            d = jnp.where(p == 0, near, jnp.where(p == 1, cross, p + 2))

            @pl.when(p != 1)
            def _():
                arrival(d, c, squares, s_send, s_recv).wait_recv()

            finish(d, c)

        if c > 0:
            finish_y(c - 1)
    finish_y(CHUNKS - 1)

    for d in range(6):
        keep_copy(d).wait_send()
        couple_copy(d).wait_send()
        for c in range(CHUNKS):
            own_copy(d, c, *own_copies).wait_send()
            own_copy(d, c, *squares_copies).wait_send()


def body(hamiltonian, keep_mask):
    blocks = hamiltonian[0, 0, 0]
    width = blocks.shape[-1]
    sizes = tuple(lax.axis_size(n) for n in ("gx", "gy", "gz"))
    keep = jnp.broadcast_to(
        keep_mask[0, 0, 0].astype(F32)[:, None, None], (7, 8, width)
    )
    count = float(sizes[0] * sizes[1] * sizes[2] * width)
    square = (width, width)
    dma = pltpu.SemaphoreType.DMA
    vmem = pltpu.VMEM
    result = pl.pallas_call(
        functools.partial(kernel, sizes, count),
        out_shape=jax.ShapeDtypeStruct((7, *square), F32),
        in_specs=[
            pl.BlockSpec(memory_space=pltpu.HBM),
            pl.BlockSpec(memory_space=vmem),
        ],
        out_specs=pl.BlockSpec(memory_space=vmem),
        scratch_shapes=[
            vmem((7, *square), F32),
            vmem((6, *square), F32),
            vmem((7, *square), F32),
            vmem((7, *square), F32),
            vmem((6, 8, width), F32),
            vmem((7, width, 3 * width), BF16),
            vmem((6, 3 * width, width), BF16),
            vmem((3 * width, width), BF16),
            vmem((width, 3 * width), BF16),
            vmem((3 * width, width), BF16),
            vmem(square, F32),
            vmem(square, F32),
            vmem((8, width), F32),
            vmem((7, 8, width), F32),
            vmem((sizes[0], 8, 128), F32),
            vmem((sizes[1], 8, 128), F32),
            vmem((sizes[2], 8, 128), F32),
            dma((7,)),
            dma((6,)),
            dma((6,)),
            dma((3,)),
            dma((3,)),
            dma((6,)),
            dma((6,)),
            dma((6, CHUNKS)),
            dma((6, CHUNKS)),
            dma((6, CHUNKS)),
            dma((6, CHUNKS)),
        ],
        compiler_params=pltpu.CompilerParams(
            collective_id=0, has_side_effects=True, vmem_limit_bytes=56 << 20
        ),
        name="sign_step",
    )(blocks, keep)
    return result[None, None, None]


def solution(mesh):
    placed = (P("gx", "gy", "gz", None, None, None), P("gx", "gy", "gz", None))
    return jax.shard_map(
        body,
        mesh=mesh,
        in_specs=placed,
        out_specs=P("gx", "gy", "gz", None, None, None),
        check_vma=False,
    )
```

time: 522 us -> 100 us (0.19); the launches traced: 513 us -> 100 us
  waiting for transfers between devices: 321 us -> 0 us
  Pallas kernels: 0 us -> 94.3 us
  blocking collectives: 81.4 us -> 0 us
  matrix products: 48.1 us -> 0 us
  starting transfers between devices: 36.4 us -> 0 us
  other arithmetic: 12.6 us -> 0.66 us
  local copies, waits for them, and re-layouts: 11.6 us -> 5.14 us
    ppermute x24 -> x0, waiting for transfers between devices: 321 us -> none  [the longest x12 215 us: passed_along(): return lax.ppermute(value, axis, pairs)]
    pallas_call x0 -> x1, Pallas kernels: none -> 94.3 us  [body(): pl.pallas_call(functools.partial(kernel, sizes, count), out_shape=jax.Sha...]
    psum x1 -> x0, blocking collectives: 81.4 us -> none  [body(): sum_total = lax.psum(own_squares, ('gx', 'gy', 'gz'))]
    dot_general x8 -> x0, matrix products: 48.1 us -> none  [the longest x2 17.2 us: product(): jnp.einsum('ij,sjk->sik', left[0], right[1:], precision=HIGHEST)]
    ppermute x24 -> x0, starting transfers between devices: 36.4 us -> none  [the longest x12 19.3 us: passed_along(): return lax.ppermute(value, axis, pairs)]
    mul x3 -> x0, other arithmetic: 5.51 us -> none  [the longest x1 2.68 us: body(): iterate = weights * (1.5 * iterate - 0.5 * cube)]
  transfers between devices with their start and end apart: 24 -> 0, of which waited for: 14 -> 0; matrix products, arithmetic and copies ran while one was open for 8% -> 0% of each run, Pallas kernels for 0% -> 0%
where the time goes in v1:
time: 100 us
  Pallas kernels  94.3 us (94%)
  local copies, waits for them, and re-layouts  5.14 us (5%)
    pallas_call x1, Pallas kernels, body(): pl.pallas_call(functools.partial(kernel, sizes, count), out_shape=jax.Sha...  94.3 us
    unnamed x1, local copies, waits for them, and re-layouts  4.42 us

profile of v1, /device:TPU:1, one launch (start us, length us, event | category | flops | bytes accessed | tf_op | source)
XLA Modules:
  0.0 100.1 jit_solution(17390508774639361888)
XLA Ops:
  0.0 0.7 convert_bitcast_fusion
  0.7 0.7 broadcast_in_dim.4.keep
  1.4 94.3 %sign_step.1 = f32[7,384,384]{2,1,0:T(8,128)} custom-call(f32[7,384,384]{2,1,0:T(8,128)} %bitcast.5, f32[7,8,384]{2,1,0:T(8,128)} %broadcast_in_dim.4.keep), custom_call_target="tpu_custom_call" | custom-call | tf_op jit(solution)/shard_map/sign_step/pallas_call | solution.py:358
  95.7 4.4 %copy.4 = f32[1,1,1,7,384,384]{5,4,3,2,1,0:T(8,128)} copy(f32[1,1,1,7,384,384]{5,4,3,2,1,0:T(8,128)} %bitcast.4) | data formatting | bytes 8257536

commit v2 on v1

--- a/solution.py
+++ b/solution.py
@@ -17,12 +17,13 @@
     sizes,
     count,
     h_hbm,
-    keep,
+    keep_in,
     out,
     h,
     near_c,
     near_o,
     squares,
+    keep,
     near_keep,
     left,
     couple,
@@ -95,6 +96,8 @@
     ]
     for load in loads:
         load.start()
+    for s in range(7):
+        keep[s] = jnp.full((8, width), keep_in[s].astype(F32))
     total = jnp.zeros((8, 128), F32)
     for s in range(7):
         loads[s].wait()
@@ -180,9 +183,9 @@
             device_id_type=MESH,
         )
 
-    def send_own(source, target, send, recv):
+    def send_own(source, target, send, recv, directions=range(6)):
         for c in range(CHUNKS):
-            for d in range(6):
+            for d in directions:
                 copy = own_copy(d, c, source, target, send, recv)
                 if d in wraps:
                     pl.when(jnp.logical_not(wraps[d]))(copy.start)
@@ -196,15 +199,6 @@
 
     squares_copies = (squares, squares, s_send, s_recv)
     own_copies = (h_hbm, near_o, o_send, o_recv)
-
-    stage_x = part_copies(0, part_x, a, peers_x)
-    for copy in stage_x:
-        copy.start()
-    for d in range(6):
-        keep_copy(d).start()
-    for d in range(6):
-        couple_copy(d).start()
-    send_own(*own_copies)
 
     def parts(x):
         high = x.astype(BF16)
@@ -234,21 +228,38 @@
     as_left(h[0], left.at[0])
     as_right(h[0], first)
 
-    @pl.loop(0, 7)
-    def _(s):
-        block = h[s]
-        as_left(block, left.at[s])
-        as_right(block, tmp_b)
-        out[s] = mul(left[0], tmp_b[...])
-
+    def own_products(low, high):
+        @pl.loop(low, high)
+        def _(s):
+            block = h[s]
+            as_left(block, left.at[s])
+            as_right(block, tmp_b)
+            out[s] = mul(left[0], tmp_b[...])
+
+    def send_parts(stage, buffer, me, peers):
+        for copy in part_copies(stage, buffer, me, peers):
+            copy.start()
+
+    def send_couples(*directions):
+        for d in directions:
+            keep_copy(d).start()
+        for d in directions:
+            couple_copy(d).start()
+
+    send_parts(0, part_x, a, peers_x)
+    send_couples(0, 1)
+    own_products(0, 2)
     part_wait(0, part_x, nx)
     part_y[g] = jnp.sum(part_x[...], axis=0)
-    for copy in part_copies(1, part_y, g, peers_y):
-        copy.start()
+    send_parts(1, part_y, g, peers_y)
+    send_couples(2, 3)
+    own_products(2, 4)
     part_wait(1, part_y, ny)
     part_z[z] = jnp.sum(part_y[...], axis=0)
-    for copy in part_copies(2, part_z, z, peers_z):
-        copy.start()
+    send_parts(2, part_z, z, peers_z)
+    send_couples(4, 5)
+    send_own(*own_copies)
+    own_products(4, 7)
 
     kept_sum[...] = jnp.zeros_like(kept_sum)
     for d in range(6):
@@ -288,22 +299,30 @@
     as_right(squares[0], tmp_b)
     centre[...] += mul(left[0], tmp_b[...])
 
-    @pl.loop(0, 6)
-    def _(p):
-        d = jnp.where(p == 0, near, jnp.where(p == 1, cross, jnp.where(p < 4, p + 2, p - 2)))
-
-        @pl.when(p != 1)
-        def _():
-            for c in range(CHUNKS):
-                arrival(d, c, near_o, o_send, o_recv).wait_recv()
-
-        as_right(near_o[1 + d], tmp_b)
-        with_own = mul(left[1 + d], tmp_b[...])
-        as_right((scale_sq[0:1] * keep[1 + d, 0:1]) * (out[1 + d] + with_own), tmp_b)
-        as_left((scale_sq[0:1] * near_keep[d, 0:1]) * with_own, tmp_a)
-        out[1 + d] = scale[1 + d, 0:1] * (1.5 * h[1 + d] - 0.5 * mul(left[0], tmp_b[...]))
-        centre[...] += mul(tmp_a[...], couple[d])
-
+    def others(low, high):
+        @pl.loop(low, high)
+        def _(p):
+            d = jnp.where(p == 0, near, jnp.where(p == 3, cross, jnp.where(p < 3, p + 3, p - 2)))
+
+            @pl.when(p != 3)
+            def _():
+                for c in range(CHUNKS):
+                    arrival(d, c, near_o, o_send, o_recv).wait_recv()
+
+            as_right(near_o[1 + d], tmp_b)
+            with_own = mul(left[1 + d], tmp_b[...])
+            as_right((scale_sq[0:1] * keep[1 + d, 0:1]) * (out[1 + d] + with_own), tmp_b)
+            as_left((scale_sq[0:1] * near_keep[d, 0:1]) * with_own, tmp_a)
+            out[1 + d] = scale[1 + d, 0:1] * (
+                1.5 * h[1 + d] - 0.5 * mul(left[0], tmp_b[...])
+            )
+            centre[...] += mul(tmp_a[...], couple[d])
+
+    others(0, 4)
+    for c in range(CHUNKS):
+        pass_chunk(c, squares, s_send, s_recv)
+        if c < 2:
+            others(4 + c, 5 + c)
     out[0] = scale[0, 0:1] * (1.5 * h[0] - 0.5 * centre[...])
 
     def finish(d, c):
@@ -313,28 +332,24 @@
             left[1 + d, :, base : base + 3 * rows], tmp_b[base : base + 3 * rows]
         )
 
-    def finish_y(c):
+    for c in range(CHUNKS):
+
+        @pl.loop(0, 4)
+        def _(p):
+            d = jnp.where(p == 0, near, jnp.where(p == 3, cross, p + 3))
+
+            @pl.when(p != 3)
+            def _():
+                arrival(d, c, squares, s_send, s_recv).wait_recv()
+
+            finish(d, c)
+
+    for c in range(CHUNKS):
+
         @pl.loop(2, 4)
         def _(d):
             arrival(d, c, squares, s_send, s_recv).wait_recv()
             finish(d, c)
-
-    for c in range(CHUNKS):
-        pass_chunk(c, squares, s_send, s_recv)
-
-        @pl.loop(0, 4)
-        def _(p):
-            d = jnp.where(p == 0, near, jnp.where(p == 1, cross, p + 2))
-
-            @pl.when(p != 1)
-            def _():
-                arrival(d, c, squares, s_send, s_recv).wait_recv()
-
-            finish(d, c)
-
-        if c > 0:
-            finish_y(c - 1)
-    finish_y(CHUNKS - 1)
 
     for d in range(6):
         keep_copy(d).wait_send()
@@ -344,23 +359,31 @@
             own_copy(d, c, *squares_copies).wait_send()
 
 
+def write_out(result, out_hbm, sem):
+    copies = [
+        pltpu.make_async_copy(result.at[s], out_hbm.at[s], sem.at[s]) for s in range(7)
+    ]
+    for copy in copies:
+        copy.start()
+    for copy in copies:
+        copy.wait()
+
+
 def body(hamiltonian, keep_mask):
     blocks = hamiltonian[0, 0, 0]
     width = blocks.shape[-1]
     sizes = tuple(lax.axis_size(n) for n in ("gx", "gy", "gz"))
-    keep = jnp.broadcast_to(
-        keep_mask[0, 0, 0].astype(F32)[:, None, None], (7, 8, width)
-    )
+    keep = keep_mask[0, 0, 0]
     count = float(sizes[0] * sizes[1] * sizes[2] * width)
     square = (width, width)
     dma = pltpu.SemaphoreType.DMA
     vmem = pltpu.VMEM
     result = pl.pallas_call(
         functools.partial(kernel, sizes, count),
-        out_shape=jax.ShapeDtypeStruct((7, *square), F32),
+        out_shape=vmem((7, *square), F32),
         in_specs=[
             pl.BlockSpec(memory_space=pltpu.HBM),
-            pl.BlockSpec(memory_space=vmem),
+            pl.BlockSpec(memory_space=pltpu.SMEM),
         ],
         out_specs=pl.BlockSpec(memory_space=vmem),
         scratch_shapes=[
@@ -368,6 +391,7 @@
             vmem((6, *square), F32),
             vmem((7, *square), F32),
             vmem((7, *square), F32),
+            vmem((7, 8, width), F32),
             vmem((6, 8, width), F32),
             vmem((7, width, 3 * width), BF16),
             vmem((6, 3 * width, width), BF16),
@@ -398,6 +422,15 @@
         ),
         name="sign_step",
     )(blocks, keep)
+    result = pl.pallas_call(
+        write_out,
+        out_shape=jax.ShapeDtypeStruct((7, *square), F32),
+        in_specs=[pl.BlockSpec(memory_space=vmem)],
+        out_specs=pl.BlockSpec(memory_space=pltpu.HBM),
+        scratch_shapes=[dma((7,))],
+        compiler_params=pltpu.CompilerParams(vmem_limit_bytes=6 << 20),
+        name="write_out",
+    )(result)
     return result[None, None, None]
 
 

time: 100 us -> 81.3 us (0.81)
  Pallas kernels: 94.3 us -> 81.2 us
  local copies, waits for them, and re-layouts: 5.14 us -> 0 us
    pallas_call x1 -> x2, Pallas kernels: 94.3 us -> 81.2 us  [the longest x1 79.2 us: body(): pl.pallas_call(functools.partial(kernel, sizes, count), out_shape=vmem((7...]
    unnamed x1 -> x0, local copies, waits for them, and re-layouts: 4.42 us -> none
where the time goes in v2:
time: 81.3 us; the launch traced here: 81.2 us
  Pallas kernels  81.2 us (100%)
    pallas_call x1, Pallas kernels, body(): pl.pallas_call(functools.partial(kernel, sizes, count), out_shape=vmem((7...  79.2 us
    pallas_call x1, Pallas kernels, body(): pl.pallas_call(write_out, out_shape=jax.ShapeDtypeStruct((7, *square), F3...  2.04 us

profile of v2, /device:TPU:1, one launch (start us, length us, event | category | flops | bytes accessed | tf_op | source)
XLA Modules:
  0.0 81.2 jit_solution(4877910080168223443)
XLA Ops:
  0.0 79.2 %sign_step.1.result = f32[7,384,384]{2,1,0:T(8,128)S(1)} custom-call(f32[7,384,384]{2,1,0:T(8,128)} %bitcast.3, s32[7]{0:T(128)} %bitcast.4), custom_call_target="tpu_custom_call" | custom-call | tf_op jit(solution)/shard_map/sign_step/pallas_call | solution.py:381
  79.2 2.0 %write_out.1 = f32[7,384,384]{2,1,0:T(8,128)} custom-call(f32[7,384,384]{2,1,0:T(8,128)S(1)} %sign_step.1.result), custom_call_target="tpu_custom_call" | custom-call | tf_op jit(solution)/shard_map/write_out/pallas_call | solution.py:425

commit v3 on v2

--- a/solution.py
+++ b/solution.py
@@ -75,7 +75,7 @@
     wraps = {2: at_top, 3: at_bottom}
 
     def chunk(c):
-        return pl.ds(c * rows, rows)
+        return pl.ds(pl.multiple_of(c * rows, rows), rows)
 
     barrier = pltpu.get_barrier_semaphore()
     peers_x = [(lax.rem(a + k, nx), g, z) for k in range(1, nx)]
@@ -228,14 +228,6 @@
     as_left(h[0], left.at[0])
     as_right(h[0], first)
 
-    def own_products(low, high):
-        @pl.loop(low, high)
-        def _(s):
-            block = h[s]
-            as_left(block, left.at[s])
-            as_right(block, tmp_b)
-            out[s] = mul(left[0], tmp_b[...])
-
     def send_parts(stage, buffer, me, peers):
         for copy in part_copies(stage, buffer, me, peers):
             copy.start()
@@ -247,21 +239,31 @@
             couple_copy(d).start()
 
     send_parts(0, part_x, a, peers_x)
-    send_couples(0, 1)
-    own_products(0, 2)
-    part_wait(0, part_x, nx)
-    part_y[g] = jnp.sum(part_x[...], axis=0)
-    send_parts(1, part_y, g, peers_y)
-    send_couples(2, 3)
-    own_products(2, 4)
-    part_wait(1, part_y, ny)
-    part_z[z] = jnp.sum(part_y[...], axis=0)
-    send_parts(2, part_z, z, peers_z)
-    send_couples(4, 5)
-    send_own(*own_copies)
-    own_products(4, 7)
+    send_couples(0, 1, 2, 3)
+
+    @pl.loop(0, 7)
+    def _(s):
+        @pl.when(s == 1)
+        def _():
+            part_wait(0, part_x, nx)
+            part_z[z] = jnp.sum(part_x[...], axis=0)
+            send_parts(1, part_z, z, peers_z)
+            send_couples(4, 5)
+
+        @pl.when(s == 4)
+        def _():
+            part_wait(1, part_z, nz)
+            part_y[g] = jnp.sum(part_z[...], axis=0)
+            send_parts(2, part_y, g, peers_y)
+            send_own(*own_copies)
+
+        block = h[s]
+        as_left(block, left.at[s])
+        as_right(block, tmp_b)
+        out[s] = mul(left[0], tmp_b[...])
 
     kept_sum[...] = jnp.zeros_like(kept_sum)
+    centre[...] = jnp.zeros_like(centre)
     for d in range(6):
         keep_copy(d).wait_recv()
 
@@ -281,75 +283,76 @@
         out[0] += both
         kept_sum[...] += near_keep[d, 0:1] * both
 
-    part_wait(2, part_z, nz)
-    norm = jnp.sum(jnp.sum(part_z[...], axis=0), keepdims=True)
+    squares[0] = keep[0, 0:1] * out[0]
+    send_own(*squares_copies)
+
+    part_wait(2, part_y, ny)
+    norm = jnp.sum(jnp.sum(part_y[...], axis=0), keepdims=True)
     norm = jnp.broadcast_to(norm, (8, width)) / count
-    factor_sq = 1.0 / norm
     factor = 1.0 / jnp.sqrt(norm)
-    scale_sq[...] = factor_sq
+    scale_sq[...] = 1.0 / norm
     for s in range(7):
         scale[s] = factor * keep[s]
-    squares[0] = (scale_sq[0:1] * keep[0, 0:1]) * out[0]
-    send_own(*squares_copies)
-
-    for c in range(CHUNKS):
-        pass_chunk(c, near_o, o_send, o_recv)
-    as_left(scale_sq[0:1] * kept_sum[...], tmp_a)
-    centre[...] = mul(tmp_a[...], first[...])
-    as_right(squares[0], tmp_b)
-    centre[...] += mul(left[0], tmp_b[...])
-
-    def others(low, high):
-        @pl.loop(low, high)
-        def _(p):
-            d = jnp.where(p == 0, near, jnp.where(p == 3, cross, jnp.where(p < 3, p + 3, p - 2)))
-
-            @pl.when(p != 3)
-            def _():
-                for c in range(CHUNKS):
-                    arrival(d, c, near_o, o_send, o_recv).wait_recv()
-
-            as_right(near_o[1 + d], tmp_b)
-            with_own = mul(left[1 + d], tmp_b[...])
-            as_right((scale_sq[0:1] * keep[1 + d, 0:1]) * (out[1 + d] + with_own), tmp_b)
-            as_left((scale_sq[0:1] * near_keep[d, 0:1]) * with_own, tmp_a)
-            out[1 + d] = scale[1 + d, 0:1] * (
-                1.5 * h[1 + d] - 0.5 * mul(left[0], tmp_b[...])
-            )
-            centre[...] += mul(tmp_a[...], couple[d])
-
-    others(0, 4)
-    for c in range(CHUNKS):
-        pass_chunk(c, squares, s_send, s_recv)
-        if c < 2:
-            others(4 + c, 5 + c)
-    out[0] = scale[0, 0:1] * (1.5 * h[0] - 0.5 * centre[...])
-
-    def finish(d, c):
-        base = 3 * c * rows
-        as_right_chunk(squares[1 + d, chunk(c)], tmp_b, base)
+
+    @pl.loop(0, 6)
+    def _(p):
+        d = jnp.where(p == 0, near, jnp.where(p == 3, cross, jnp.where(p < 3, p + 3, p - 2)))
+
+        @pl.when(p == 2)
+        def _():
+            as_left(scale_sq[0:1] * kept_sum[...], tmp_a)
+            centre[...] += mul(tmp_a[...], first[...])
+            as_right(scale_sq[0:1] * squares[0], tmp_b)
+            centre[...] += mul(left[0], tmp_b[...])
+
+        @pl.when(p < CHUNKS)
+        def _():
+            pass_chunk(p, near_o, o_send, o_recv)
+
+        @pl.when(p > 3)
+        def _():
+            pass_chunk(p - 4, squares, s_send, s_recv)
+
+        @pl.when(p != 3)
+        def _():
+            for c in range(CHUNKS):
+                arrival(d, c, near_o, o_send, o_recv).wait_recv()
+
+        as_right(near_o[1 + d], tmp_b)
+        with_own = mul(left[1 + d], tmp_b[...])
+        as_right((scale_sq[0:1] * keep[1 + d, 0:1]) * (out[1 + d] + with_own), tmp_b)
+        as_left((scale_sq[0:1] * near_keep[d, 0:1]) * with_own, tmp_a)
+        out[1 + d] = scale[1 + d, 0:1] * (
+            1.5 * h[1 + d] - 0.5 * mul(left[0], tmp_b[...])
+        )
+        centre[...] += mul(tmp_a[...], couple[d])
+
+    @pl.loop(0, 4)
+    def _(p):
+        d = jnp.where(p == 0, near, jnp.where(p == 3, cross, p + 3))
+
+        @pl.when(p == 1)
+        def _():
+            pass_chunk(CHUNKS - 1, squares, s_send, s_recv)
+            out[0] = scale[0, 0:1] * (1.5 * h[0] - 0.5 * centre[...])
+
+        @pl.when(p != 3)
+        def _():
+            for c in range(CHUNKS):
+                arrival(d, c, squares, s_send, s_recv).wait_recv()
+
+        as_right(scale_sq[0:1] * squares[1 + d], tmp_b)
+        out[1 + d] -= (0.5 * scale[1 + d, 0:1]) * mul(left[1 + d], tmp_b[...])
+
+    @pl.loop(0, 2 * CHUNKS)
+    def _(q):
+        d, c = 2 + lax.rem(q, 2), q // 2
+        arrival(d, c, squares, s_send, s_recv).wait_recv()
+        as_right_chunk(scale_sq[0:1] * squares[1 + d, chunk(c)], tmp_b, 0)
+        columns = pl.ds(pl.multiple_of(3 * c * rows, 3 * rows), 3 * rows)
         out[1 + d] -= (0.5 * scale[1 + d, 0:1]) * mul(
-            left[1 + d, :, base : base + 3 * rows], tmp_b[base : base + 3 * rows]
-        )
-
-    for c in range(CHUNKS):
-
-        @pl.loop(0, 4)
-        def _(p):
-            d = jnp.where(p == 0, near, jnp.where(p == 3, cross, p + 3))
-
-            @pl.when(p != 3)
-            def _():
-                arrival(d, c, squares, s_send, s_recv).wait_recv()
-
-            finish(d, c)
-
-    for c in range(CHUNKS):
-
-        @pl.loop(2, 4)
-        def _(d):
-            arrival(d, c, squares, s_send, s_recv).wait_recv()
-            finish(d, c)
+            left[1 + d, :, columns], tmp_b[0 : 3 * rows]
+        )
 
     for d in range(6):
         keep_copy(d).wait_send()

time: 81.3 us -> 77.2 us (0.950)
  Pallas kernels: 81.2 us -> 77.1 us
    pallas_call x1, Pallas kernels: 79.2 us -> 75 us  [body(): pl.pallas_call(functools.partial(kernel, sizes, count), out_shape=vmem((7...]
where the time goes in v3:
time: 77.2 us; the launch traced here: 77.1 us
  Pallas kernels  77.1 us (100%)
    pallas_call x1, Pallas kernels, body(): pl.pallas_call(functools.partial(kernel, sizes, count), out_shape=vmem((7...  75 us
    pallas_call x1, Pallas kernels, body(): pl.pallas_call(write_out, out_shape=jax.ShapeDtypeStruct((7, *square), F3...  2.04 us

profile of v3, /device:TPU:1, one launch (start us, length us, event | category | flops | bytes accessed | tf_op | source)
XLA Modules:
  0.0 77.1 jit_solution(797368276234733747)
XLA Ops:
  0.0 75.0 %sign_step.1.result = f32[7,384,384]{2,1,0:T(8,128)S(1)} custom-call(f32[7,384,384]{2,1,0:T(8,128)} %bitcast.3, s32[7]{0:T(128)} %bitcast.4), custom_call_target="tpu_custom_call" | custom-call | tf_op jit(solution)/shard_map/sign_step/pallas_call | solution.py:384
  75.0 2.0 %write_out.1 = f32[7,384,384]{2,1,0:T(8,128)} custom-call(f32[7,384,384]{2,1,0:T(8,128)S(1)} %sign_step.1.result), custom_call_target="tpu_custom_call" | custom-call | tf_op jit(solution)/shard_map/write_out/pallas_call | solution.py:428

commit v4 on v3

--- a/solution.py
+++ b/solution.py
@@ -25,6 +25,7 @@
     squares,
     keep,
     near_keep,
+    relay,
     left,
     couple,
     first,
@@ -44,6 +45,8 @@
     part_recv,
     c_send,
     c_recv,
+    relay_send,
+    relay_recv,
     o_send,
     o_recv,
     s_send,
@@ -73,6 +76,10 @@
     near = 1 - cross
     passed_on = {2: (across, up_y, z), 3: (across, down_y, z)}
     wraps = {2: at_top, 3: at_bottom}
+    even = lax.rem(a, 2) == 0
+    relays = even & jnp.logical_not(edge)
+    above = lax.rem(g, half) == half - 2
+    relay_to = (a, lax.rem(g + jnp.where(above, 2, ny - 2), ny), z)
 
     def chunk(c):
         return pl.ds(pl.multiple_of(c * rows, rows), rows)
@@ -153,6 +160,26 @@
             device_id_type=MESH,
         )
 
+    def to_relay(d, c):
+        return pltpu.make_async_remote_copy(
+            src_ref=h_hbm.at[1 + d, chunk(c)],
+            dst_ref=relay.at[chunk(c)],
+            send_sem=c_send.at[d],
+            recv_sem=relay_recv.at[c],
+            device_id=device[d ^ 1],
+            device_id_type=MESH,
+        )
+
+    def from_relay(c):
+        return pltpu.make_async_remote_copy(
+            src_ref=relay.at[chunk(c)],
+            dst_ref=near_c.at[jnp.where(above, 3, 2), chunk(c)],
+            send_sem=relay_send.at[0],
+            recv_sem=c_recv.at[jnp.where(above, 3, 2)],
+            device_id=relay_to,
+            device_id_type=MESH,
+        )
+
     def own_copy(d, c, source, target, send, recv):
         return pltpu.make_async_remote_copy(
             src_ref=source.at[0, chunk(c)],
@@ -236,7 +263,19 @@
         for d in directions:
             keep_copy(d).start()
         for d in directions:
-            couple_copy(d).start()
+            if d in wraps:
+
+                @pl.when(wraps[d] & even)
+                def _():
+                    for c in range(CHUNKS):
+                        to_relay(d, c).start()
+
+                pl.when(wraps[d] & jnp.logical_not(even))(couple_copy(d).start)
+        for d in directions:
+            if d in wraps:
+                pl.when(jnp.logical_not(wraps[d]))(couple_copy(d).start)
+            else:
+                couple_copy(d).start()
 
     send_parts(0, part_x, a, peers_x)
     send_couples(0, 1, 2, 3)
@@ -255,12 +294,20 @@
             part_wait(1, part_z, nz)
             part_y[g] = jnp.sum(part_z[...], axis=0)
             send_parts(2, part_y, g, peers_y)
-            send_own(*own_copies)
+            send_own(*own_copies, range(2, 6))
 
         block = h[s]
         as_left(block, left.at[s])
         as_right(block, tmp_b)
         out[s] = mul(left[0], tmp_b[...])
+
+    @pl.when(relays)
+    def _():
+        for c in range(CHUNKS):
+            to_relay(0, c).wait_recv()
+            from_relay(c).start()
+
+    send_own(*own_copies, range(2))
 
     kept_sum[...] = jnp.zeros_like(kept_sum)
     centre[...] = jnp.zeros_like(centre)
@@ -353,6 +400,17 @@
         out[1 + d] -= (0.5 * scale[1 + d, 0:1]) * mul(
             left[1 + d, :, columns], tmp_b[0 : 3 * rows]
         )
+
+    @pl.when(relays)
+    def _():
+        pltpu.make_async_remote_copy(
+            src_ref=relay,
+            dst_ref=relay,
+            send_sem=relay_send.at[0],
+            recv_sem=relay_recv.at[0],
+            device_id=relay_to,
+            device_id_type=MESH,
+        ).wait_send()
 
     for d in range(6):
         keep_copy(d).wait_send()
@@ -396,6 +454,7 @@
             vmem((7, *square), F32),
             vmem((7, 8, width), F32),
             vmem((6, 8, width), F32),
+            vmem(square, F32),
             vmem((7, width, 3 * width), BF16),
             vmem((6, 3 * width, width), BF16),
             vmem((3 * width, width), BF16),
@@ -415,6 +474,8 @@
             dma((3,)),
             dma((6,)),
             dma((6,)),
+            dma((1,)),
+            dma((CHUNKS,)),
             dma((6, CHUNKS)),
             dma((6, CHUNKS)),
             dma((6, CHUNKS)),

time: 77.2 us -> 71.4 us (0.925)
  the two profiles are of different devices: /device:TPU:1 before, /device:TPU:6 now
where the time goes in v4:
time: 71.4 us; the launch traced here: 71.3 us
  Pallas kernels  71.3 us (100%)
    pallas_call x1, Pallas kernels, body(): pl.pallas_call(functools.partial(kernel, sizes, count), out_shape=vmem((7...  69.3 us
    pallas_call x1, Pallas kernels, body(): pl.pallas_call(write_out, out_shape=jax.ShapeDtypeStruct((7, *square), F3...  2.04 us

profile of v4, /device:TPU:6, one launch (start us, length us, event | category | flops | bytes accessed | tf_op | source)
XLA Modules:
  0.0 71.3 jit_solution(11781787710948819362)
XLA Ops:
  0.0 69.3 %sign_step.1.result = f32[7,384,384]{2,1,0:T(8,128)S(1)} custom-call(f32[7,384,384]{2,1,0:T(8,128)} %bitcast.3, s32[7]{0:T(128)} %bitcast.4), custom_call_target="tpu_custom_call" | custom-call | tf_op jit(solution)/shard_map/sign_step/pallas_call | solution.py:442
  69.3 2.0 %write_out.1 = f32[7,384,384]{2,1,0:T(8,128)} custom-call(f32[7,384,384]{2,1,0:T(8,128)S(1)} %sign_step.1.result), custom_call_target="tpu_custom_call" | custom-call | tf_op jit(solution)/shard_map/write_out/pallas_call | solution.py:489

commit v5 on v4

--- a/solution.py
+++ b/solution.py
@@ -11,6 +11,7 @@
 F32 = jnp.float32
 BF16 = jnp.bfloat16
 CHUNKS = 3
+PIECES = 6
 
 
 def kernel(
@@ -77,12 +78,16 @@
     passed_on = {2: (across, up_y, z), 3: (across, down_y, z)}
     wraps = {2: at_top, 3: at_bottom}
     even = lax.rem(a, 2) == 0
-    relays = even & jnp.logical_not(edge)
+    inner = jnp.logical_not(edge)
     above = lax.rem(g, half) == half - 2
     relay_to = (a, lax.rem(g + jnp.where(above, 2, ny - 2), ny), z)
 
     def chunk(c):
         return pl.ds(pl.multiple_of(c * rows, rows), rows)
+
+    def piece(c):
+        size = width // PIECES
+        return pl.ds(pl.multiple_of(c * size, size), size)
 
     barrier = pltpu.get_barrier_semaphore()
     peers_x = [(lax.rem(a + k, nx), g, z) for k in range(1, nx)]
@@ -170,11 +175,21 @@
             device_id_type=MESH,
         )
 
+    def to_wrap(d, c):
+        return pltpu.make_async_remote_copy(
+            src_ref=h_hbm.at[1 + d, chunk(c)],
+            dst_ref=near_c.at[d ^ 1, chunk(c)],
+            send_sem=c_send.at[d],
+            recv_sem=c_recv.at[d ^ 1],
+            device_id=device[d],
+            device_id_type=MESH,
+        )
+
     def from_relay(c):
         return pltpu.make_async_remote_copy(
             src_ref=relay.at[chunk(c)],
             dst_ref=near_c.at[jnp.where(above, 3, 2), chunk(c)],
-            send_sem=relay_send.at[0],
+            send_sem=relay_send.at[min(c, 1)],
             recv_sem=c_recv.at[jnp.where(above, 3, 2)],
             device_id=relay_to,
             device_id_type=MESH,
@@ -182,8 +197,8 @@
 
     def own_copy(d, c, source, target, send, recv):
         return pltpu.make_async_remote_copy(
-            src_ref=source.at[0, chunk(c)],
-            dst_ref=target.at[1 + (d ^ 1), chunk(c)],
+            src_ref=source.at[0, piece(c)],
+            dst_ref=target.at[1 + (d ^ 1), piece(c)],
             send_sem=send.at[d, c],
             recv_sem=recv.at[d ^ 1, c],
             device_id=device[d],
@@ -192,8 +207,8 @@
 
     def pass_copy(d, c, target, send, recv):
         return pltpu.make_async_remote_copy(
-            src_ref=target.at[1 + cross, chunk(c)],
-            dst_ref=target.at[1 + (d ^ 1), chunk(c)],
+            src_ref=target.at[1 + cross, piece(c)],
+            dst_ref=target.at[1 + (d ^ 1), piece(c)],
             send_sem=send.at[d, c],
             recv_sem=recv.at[d ^ 1, c],
             device_id=passed_on[d],
@@ -202,8 +217,8 @@
 
     def arrival(d, c, target, send, recv):
         return pltpu.make_async_remote_copy(
-            src_ref=target.at[1 + d, chunk(c)],
-            dst_ref=target.at[1 + d, chunk(c)],
+            src_ref=target.at[1 + d, piece(c)],
+            dst_ref=target.at[1 + d, piece(c)],
             send_sem=send.at[0, c],
             recv_sem=recv.at[d, c],
             device_id=device[0],
@@ -211,7 +226,7 @@
         )
 
     def send_own(source, target, send, recv, directions=range(6)):
-        for c in range(CHUNKS):
+        for c in range(PIECES):
             for d in directions:
                 copy = own_copy(d, c, source, target, send, recv)
                 if d in wraps:
@@ -219,7 +234,7 @@
                 else:
                     copy.start()
 
-    def pass_chunk(c, target, send, recv):
+    def pass_piece(c, target, send, recv):
         arrival(cross, c, target, send, recv).wait_recv()
         for d in (2, 3):
             pl.when(wraps[d])(pass_copy(d, c, target, send, recv).start)
@@ -265,12 +280,12 @@
         for d in directions:
             if d in wraps:
 
-                @pl.when(wraps[d] & even)
-                def _():
-                    for c in range(CHUNKS):
-                        to_relay(d, c).start()
-
-                pl.when(wraps[d] & jnp.logical_not(even))(couple_copy(d).start)
+                for c in range(CHUNKS):
+                    if c == 0:
+                        pl.when(wraps[d])(to_relay(d, c).start)
+                    else:
+                        pl.when(wraps[d] & even)(to_relay(d, c).start)
+                        pl.when(wraps[d] & jnp.logical_not(even))(to_wrap(d, c).start)
         for d in directions:
             if d in wraps:
                 pl.when(jnp.logical_not(wraps[d]))(couple_copy(d).start)
@@ -301,13 +316,17 @@
         as_right(block, tmp_b)
         out[s] = mul(left[0], tmp_b[...])
 
-    @pl.when(relays)
-    def _():
-        for c in range(CHUNKS):
+    def relay_chunks(*chunks):
+        for c in chunks:
             to_relay(0, c).wait_recv()
             from_relay(c).start()
 
-    send_own(*own_copies, range(2))
+    pl.when(inner)(functools.partial(relay_chunks, 0))
+    pl.when(inner & even)(functools.partial(relay_chunks, *range(1, CHUNKS)))
+
+    @pl.when(edge)
+    def _():
+        send_own(*own_copies, range(2))
 
     kept_sum[...] = jnp.zeros_like(kept_sum)
     centre[...] = jnp.zeros_like(centre)
@@ -316,7 +335,17 @@
 
     @pl.loop(0, 6)
     def _(p):
-        d = jnp.where(p == 0, near, jnp.where(p == 5, cross, jnp.where(p < 3, p + 3, p - 1)))
+        d = jnp.where(p == 0, near, jnp.where(p == 3, cross, jnp.where(p < 3, p + 3, p - 2)))
+
+        @pl.when((p == 3) & jnp.logical_not(edge))
+        def _():
+            send_own(*own_copies, range(2))
+
+        @pl.when(p == 5)
+        def _():
+            pass_piece(0, near_o, o_send, o_recv)
+            pass_piece(1, near_o, o_send, o_recv)
+
         pltpu.make_async_remote_copy(
             src_ref=near_c.at[d],
             dst_ref=near_c.at[d],
@@ -345,24 +374,29 @@
     def _(p):
         d = jnp.where(p == 0, near, jnp.where(p == 3, cross, jnp.where(p < 3, p + 3, p - 2)))
 
-        @pl.when(p == 2)
+        @pl.when(p < 2)
+        def _():
+            pass_piece(2 * p + 2, near_o, o_send, o_recv)
+            pass_piece(2 * p + 3, near_o, o_send, o_recv)
+
+        @pl.when(p == 1)
         def _():
             as_left(scale_sq[0:1] * kept_sum[...], tmp_a)
             centre[...] += mul(tmp_a[...], first[...])
             as_right(scale_sq[0:1] * squares[0], tmp_b)
             centre[...] += mul(left[0], tmp_b[...])
 
-        @pl.when(p < CHUNKS)
-        def _():
-            pass_chunk(p, near_o, o_send, o_recv)
-
-        @pl.when(p > 3)
-        def _():
-            pass_chunk(p - 4, squares, s_send, s_recv)
+        @pl.when(p == 3)
+        def _():
+            pass_piece(0, squares, s_send, s_recv)
+
+        @pl.when(p >= 3)
+        def _():
+            pass_piece(p - 2, squares, s_send, s_recv)
 
         @pl.when(p != 3)
         def _():
-            for c in range(CHUNKS):
+            for c in range(PIECES):
                 arrival(d, c, near_o, o_send, o_recv).wait_recv()
 
         as_right(near_o[1 + d], tmp_b)
@@ -378,14 +412,17 @@
     def _(p):
         d = jnp.where(p == 0, near, jnp.where(p == 3, cross, p + 3))
 
+        @pl.when(p < 2)
+        def _():
+            pass_piece(4 + p, squares, s_send, s_recv)
+
         @pl.when(p == 1)
         def _():
-            pass_chunk(CHUNKS - 1, squares, s_send, s_recv)
             out[0] = scale[0, 0:1] * (1.5 * h[0] - 0.5 * centre[...])
 
         @pl.when(p != 3)
         def _():
-            for c in range(CHUNKS):
+            for c in range(PIECES):
                 arrival(d, c, squares, s_send, s_recv).wait_recv()
 
         as_right(scale_sq[0:1] * squares[1 + d], tmp_b)
@@ -394,28 +431,34 @@
     @pl.loop(0, 2 * CHUNKS)
     def _(q):
         d, c = 2 + lax.rem(q, 2), q // 2
-        arrival(d, c, squares, s_send, s_recv).wait_recv()
+        for k in range(PIECES // CHUNKS):
+            arrival(
+                d, PIECES // CHUNKS * c + k, squares, s_send, s_recv
+            ).wait_recv()
         as_right_chunk(scale_sq[0:1] * squares[1 + d, chunk(c)], tmp_b, 0)
         columns = pl.ds(pl.multiple_of(3 * c * rows, 3 * rows), 3 * rows)
         out[1 + d] -= (0.5 * scale[1 + d, 0:1]) * mul(
             left[1 + d, :, columns], tmp_b[0 : 3 * rows]
         )
 
-    @pl.when(relays)
-    def _():
+    def relay_left(first, n):
+        part = relay.at[pl.ds(first * rows, n * rows)]
         pltpu.make_async_remote_copy(
-            src_ref=relay,
-            dst_ref=relay,
-            send_sem=relay_send.at[0],
-            recv_sem=relay_recv.at[0],
+            src_ref=part,
+            dst_ref=part,
+            send_sem=relay_send.at[first],
+            recv_sem=relay_recv.at[first],
             device_id=relay_to,
             device_id_type=MESH,
         ).wait_send()
+
+    pl.when(inner)(functools.partial(relay_left, 0, 1))
+    pl.when(inner & even)(functools.partial(relay_left, 1, CHUNKS - 1))
 
     for d in range(6):
         keep_copy(d).wait_send()
         couple_copy(d).wait_send()
-        for c in range(CHUNKS):
+        for c in range(PIECES):
             own_copy(d, c, *own_copies).wait_send()
             own_copy(d, c, *squares_copies).wait_send()
 
@@ -474,12 +517,12 @@
             dma((3,)),
             dma((6,)),
             dma((6,)),
-            dma((1,)),
+            dma((2,)),
             dma((CHUNKS,)),
-            dma((6, CHUNKS)),
-            dma((6, CHUNKS)),
-            dma((6, CHUNKS)),
-            dma((6, CHUNKS)),
+            dma((6, PIECES)),
+            dma((6, PIECES)),
+            dma((6, PIECES)),
+            dma((6, PIECES)),
         ],
         compiler_params=pltpu.CompilerParams(
             collective_id=0, has_side_effects=True, vmem_limit_bytes=56 << 20

time: 71.4 us -> 68.2 us (0.955)
  the two profiles are of different devices: /device:TPU:6 before, /device:TPU:1 now
where the time goes in v5:
time: 68.2 us; the launch traced here: 68.1 us
  Pallas kernels  68.1 us (100%)
    pallas_call x1, Pallas kernels, body(): pl.pallas_call(functools.partial(kernel, sizes, count), out_shape=vmem((7...  66 us
    pallas_call x1, Pallas kernels, body(): pl.pallas_call(write_out, out_shape=jax.ShapeDtypeStruct((7, *square), F3...  2.04 us

profile of v5, /device:TPU:1, one launch (start us, length us, event | category | flops | bytes accessed | tf_op | source)
XLA Modules:
  0.0 68.1 jit_solution(5187847372674585893)
XLA Ops:
  0.0 66.0 %sign_step.1.result = f32[7,384,384]{2,1,0:T(8,128)S(1)} custom-call(f32[7,384,384]{2,1,0:T(8,128)} %bitcast.3, s32[7]{0:T(128)} %bitcast.4), custom_call_target="tpu_custom_call" | custom-call | tf_op jit(solution)/shard_map/sign_step/pallas_call | solution.py:485
  66.0 2.0 %write_out.1 = f32[7,384,384]{2,1,0:T(8,128)} custom-call(f32[7,384,384]{2,1,0:T(8,128)S(1)} %sign_step.1.result), custom_call_target="tpu_custom_call" | custom-call | tf_op jit(solution)/shard_map/write_out/pallas_call | solution.py:532

commit v6 on v5

--- a/solution.py
+++ b/solution.py
@@ -77,6 +77,12 @@
     near = 1 - cross
     passed_on = {2: (across, up_y, z), 3: (across, down_y, z)}
     wraps = {2: at_top, 3: at_bottom}
+    wrapped = jnp.where(at_top, 2, 3)
+    late = [
+        jnp.where(edge, cross, 2),
+        jnp.where(edge, 5 - wrapped, 3),
+        jnp.where(edge, wrapped, cross),
+    ]
     even = lax.rem(a, 2) == 0
     inner = jnp.logical_not(edge)
     above = lax.rem(g, half) == half - 2
@@ -234,6 +240,9 @@
                 else:
                     copy.start()
 
+    def awaits(d):
+        return jnp.logical_not(edge & (d == cross))
+
     def pass_piece(c, target, send, recv):
         arrival(cross, c, target, send, recv).wait_recv()
         for d in (2, 3):
@@ -328,6 +337,12 @@
     def _():
         send_own(*own_copies, range(2))
 
+    def direction(p):
+        d = jnp.where(p == 0, near, p + 3)
+        for k in range(3):
+            d = jnp.where(p == 3 + k, late[k], d)
+        return d
+
     kept_sum[...] = jnp.zeros_like(kept_sum)
     centre[...] = jnp.zeros_like(centre)
     for d in range(6):
@@ -335,13 +350,13 @@
 
     @pl.loop(0, 6)
     def _(p):
-        d = jnp.where(p == 0, near, jnp.where(p == 3, cross, jnp.where(p < 3, p + 3, p - 2)))
+        d = direction(p)
 
         @pl.when((p == 3) & jnp.logical_not(edge))
         def _():
             send_own(*own_copies, range(2))
 
-        @pl.when(p == 5)
+        @pl.when((p == 5) & edge)
         def _():
             pass_piece(0, near_o, o_send, o_recv)
             pass_piece(1, near_o, o_send, o_recv)
@@ -372,9 +387,9 @@
 
     @pl.loop(0, 6)
     def _(p):
-        d = jnp.where(p == 0, near, jnp.where(p == 3, cross, jnp.where(p < 3, p + 3, p - 2)))
-
-        @pl.when(p < 2)
+        d = direction(p)
+
+        @pl.when((p < 2) & edge)
         def _():
             pass_piece(2 * p + 2, near_o, o_send, o_recv)
             pass_piece(2 * p + 3, near_o, o_send, o_recv)
@@ -386,15 +401,15 @@
             as_right(scale_sq[0:1] * squares[0], tmp_b)
             centre[...] += mul(left[0], tmp_b[...])
 
-        @pl.when(p == 3)
+        @pl.when((p == 3) & edge)
         def _():
             pass_piece(0, squares, s_send, s_recv)
 
-        @pl.when(p >= 3)
+        @pl.when((p >= 3) & edge)
         def _():
             pass_piece(p - 2, squares, s_send, s_recv)
 
-        @pl.when(p != 3)
+        @pl.when(awaits(d))
         def _():
             for c in range(PIECES):
                 arrival(d, c, near_o, o_send, o_recv).wait_recv()
@@ -410,9 +425,10 @@
 
     @pl.loop(0, 4)
     def _(p):
-        d = jnp.where(p == 0, near, jnp.where(p == 3, cross, p + 3))
-
-        @pl.when(p < 2)
+        d = jnp.where(p == 0, near, p + 3)
+        d = jnp.where(p == 3, jnp.where(edge, late[1], late[0]), d)
+
+        @pl.when((p < 2) & edge)
         def _():
             pass_piece(4 + p, squares, s_send, s_recv)
 
@@ -420,21 +436,24 @@
         def _():
             out[0] = scale[0, 0:1] * (1.5 * h[0] - 0.5 * centre[...])
 
-        @pl.when(p != 3)
-        def _():
-            for c in range(PIECES):
-                arrival(d, c, squares, s_send, s_recv).wait_recv()
+        for c in range(PIECES):
+            arrival(d, c, squares, s_send, s_recv).wait_recv()
 
         as_right(scale_sq[0:1] * squares[1 + d], tmp_b)
         out[1 + d] -= (0.5 * scale[1 + d, 0:1]) * mul(left[1 + d], tmp_b[...])
 
     @pl.loop(0, 2 * CHUNKS)
     def _(q):
-        d, c = 2 + lax.rem(q, 2), q // 2
-        for k in range(PIECES // CHUNKS):
-            arrival(
-                d, PIECES // CHUNKS * c + k, squares, s_send, s_recv
-            ).wait_recv()
+        earlier = jnp.where(edge, late[0], late[1])
+        d, c = jnp.where(lax.rem(q, 2) == 0, earlier, late[2]), q // 2
+
+        @pl.when(awaits(d))
+        def _():
+            for k in range(PIECES // CHUNKS):
+                arrival(
+                    d, PIECES // CHUNKS * c + k, squares, s_send, s_recv
+                ).wait_recv()
+
         as_right_chunk(scale_sq[0:1] * squares[1 + d, chunk(c)], tmp_b, 0)
         columns = pl.ds(pl.multiple_of(3 * c * rows, 3 * rows), 3 * rows)
         out[1 + d] -= (0.5 * scale[1 + d, 0:1]) * mul(

time: 68.2 us -> 67.4 us (0.988)
  Pallas kernels: 68.1 us -> 67.3 us
    pallas_call x1, Pallas kernels: 66 us -> 65.3 us  [body(): pl.pallas_call(functools.partial(kernel, sizes, count), out_shape=vmem((7...]
where the time goes in v6:
time: 67.4 us; the launch traced here: 67.3 us
  Pallas kernels  67.3 us (100%)
    pallas_call x1, Pallas kernels, body(): pl.pallas_call(functools.partial(kernel, sizes, count), out_shape=vmem((7...  65.3 us
    pallas_call x1, Pallas kernels, body(): pl.pallas_call(write_out, out_shape=jax.ShapeDtypeStruct((7, *square), F3...  2.04 us

profile of v6, /device:TPU:1, one launch (start us, length us, event | category | flops | bytes accessed | tf_op | source)
XLA Modules:
  0.0 67.3 jit_solution(8122474395611665564)
XLA Ops:
  0.0 65.3 %sign_step.1.result = f32[7,384,384]{2,1,0:T(8,128)S(1)} custom-call(f32[7,384,384]{2,1,0:T(8,128)} %bitcast.3, s32[7]{0:T(128)} %bitcast.4), custom_call_target="tpu_custom_call" | custom-call | tf_op jit(solution)/shard_map/sign_step/pallas_call | solution.py:504
  65.3 2.0 %write_out.1 = f32[7,384,384]{2,1,0:T(8,128)} custom-call(f32[7,384,384]{2,1,0:T(8,128)S(1)} %sign_step.1.result), custom_call_target="tpu_custom_call" | custom-call | tf_op jit(solution)/shard_map/write_out/pallas_call | solution.py:551

commit v7 on v6

--- a/solution.py
+++ b/solution.py
@@ -205,7 +205,7 @@
         return pltpu.make_async_remote_copy(
             src_ref=source.at[0, piece(c)],
             dst_ref=target.at[1 + (d ^ 1), piece(c)],
-            send_sem=send.at[d, c],
+            send_sem=send.at[d],
             recv_sem=recv.at[d ^ 1, c],
             device_id=device[d],
             device_id_type=MESH,
@@ -215,7 +215,7 @@
         return pltpu.make_async_remote_copy(
             src_ref=target.at[1 + cross, piece(c)],
             dst_ref=target.at[1 + (d ^ 1), piece(c)],
-            send_sem=send.at[d, c],
+            send_sem=send.at[d],
             recv_sem=recv.at[d ^ 1, c],
             device_id=passed_on[d],
             device_id_type=MESH,
@@ -225,7 +225,7 @@
         return pltpu.make_async_remote_copy(
             src_ref=target.at[1 + d, piece(c)],
             dst_ref=target.at[1 + d, piece(c)],
-            send_sem=send.at[0, c],
+            send_sem=send.at[0],
             recv_sem=recv.at[d, c],
             device_id=device[0],
             device_id_type=MESH,
@@ -442,22 +442,14 @@
         as_right(scale_sq[0:1] * squares[1 + d], tmp_b)
         out[1 + d] -= (0.5 * scale[1 + d, 0:1]) * mul(left[1 + d], tmp_b[...])
 
-    @pl.loop(0, 2 * CHUNKS)
-    def _(q):
-        earlier = jnp.where(edge, late[0], late[1])
-        d, c = jnp.where(lax.rem(q, 2) == 0, earlier, late[2]), q // 2
-
-        @pl.when(awaits(d))
-        def _():
-            for k in range(PIECES // CHUNKS):
-                arrival(
-                    d, PIECES // CHUNKS * c + k, squares, s_send, s_recv
-                ).wait_recv()
-
-        as_right_chunk(scale_sq[0:1] * squares[1 + d, chunk(c)], tmp_b, 0)
-        columns = pl.ds(pl.multiple_of(3 * c * rows, 3 * rows), 3 * rows)
-        out[1 + d] -= (0.5 * scale[1 + d, 0:1]) * mul(
-            left[1 + d, :, columns], tmp_b[0 : 3 * rows]
+    def sent(d, source, target, send, recv):
+        return pltpu.make_async_remote_copy(
+            src_ref=source.at[0],
+            dst_ref=target.at[1 + (d ^ 1)],
+            send_sem=send.at[d],
+            recv_sem=recv.at[d ^ 1, 0],
+            device_id=device[d],
+            device_id_type=MESH,
         )
 
     def relay_left(first, n):
@@ -477,9 +469,28 @@
     for d in range(6):
         keep_copy(d).wait_send()
         couple_copy(d).wait_send()
-        for c in range(PIECES):
-            own_copy(d, c, *own_copies).wait_send()
-            own_copy(d, c, *squares_copies).wait_send()
+        sent(d, *own_copies).wait_send()
+
+    @pl.loop(0, 2 * CHUNKS)
+    def _(q):
+        earlier = jnp.where(edge, late[0], late[1])
+        d, c = jnp.where(lax.rem(q, 2) == 0, earlier, late[2]), q // 2
+
+        @pl.when(awaits(d))
+        def _():
+            for k in range(PIECES // CHUNKS):
+                arrival(
+                    d, PIECES // CHUNKS * c + k, squares, s_send, s_recv
+                ).wait_recv()
+
+        as_right_chunk(scale_sq[0:1] * squares[1 + d, chunk(c)], tmp_b, 0)
+        columns = pl.ds(pl.multiple_of(3 * c * rows, 3 * rows), 3 * rows)
+        out[1 + d] -= (0.5 * scale[1 + d, 0:1]) * mul(
+            left[1 + d, :, columns], tmp_b[0 : 3 * rows]
+        )
+
+    for d in range(6):
+        sent(d, *squares_copies).wait_send()
 
 
 def write_out(result, out_hbm, sem):
@@ -538,9 +549,9 @@
             dma((6,)),
             dma((2,)),
             dma((CHUNKS,)),
+            dma((6,)),
             dma((6, PIECES)),
-            dma((6, PIECES)),
-            dma((6, PIECES)),
+            dma((6,)),
             dma((6, PIECES)),
         ],
         compiler_params=pltpu.CompilerParams(

time: 67.4 us -> 66.7 us (0.990)
  Pallas kernels: 67.3 us -> 66.6 us
where the time goes in v7:
time: 66.7 us
  Pallas kernels  66.6 us (100%)
    pallas_call x1, Pallas kernels, body(): pl.pallas_call(functools.partial(kernel, sizes, count), out_shape=vmem((7...  64.6 us
    pallas_call x1, Pallas kernels, body(): pl.pallas_call(write_out, out_shape=jax.ShapeDtypeStruct((7, *square), F3...  2.04 us

profile of v7, /device:TPU:1, one launch (start us, length us, event | category | flops | bytes accessed | tf_op | source)
XLA Modules:
  0.0 66.7 jit_solution(26195887454623565)
XLA Ops:
  0.0 64.6 %sign_step.1.result = f32[7,384,384]{2,1,0:T(8,128)S(1)} custom-call(f32[7,384,384]{2,1,0:T(8,128)} %bitcast.3, s32[7]{0:T(128)} %bitcast.4), custom_call_target="tpu_custom_call" | custom-call | tf_op jit(solution)/shard_map/sign_step/pallas_call | solution.py:515
  64.6 2.0 %write_out.1 = f32[7,384,384]{2,1,0:T(8,128)} custom-call(f32[7,384,384]{2,1,0:T(8,128)S(1)} %sign_step.1.result), custom_call_target="tpu_custom_call" | custom-call | tf_op jit(solution)/shard_map/write_out/pallas_call | solution.py:562
